TPU v7x, 32 devices: a whole 2x2x4 slice. The times are simulated.
32 devices in a mesh: section: 2 (over x), space: 16 (over z, y, core).
Axes of the slice: x: 2, y: 2, z: 4, core: 2. Of those that a mesh axis runs over, the one named last changes fastest.
Arguments:
- input_tiles: bfloat16 [16, 2, 4, 8, 8, 256], P('space'), may hold values from -6 to 6
- saved_tiles: bfloat16 [16, 2, 32, 4, 4, 128], P('space'), may hold values from -6 to 6
- out_grad_tiles: bfloat16 [16, 2, 64, 2, 2, 64], P('space'), may hold values from -1 to 1
- kernel_first: bfloat16 [32, 4, 3, 3, 3], replicated, may hold values from -0.625 to 0.625
- bias_first: float32 [32], replicated, may hold values from -3 to 3
- kernel_second: bfloat16 [64, 32, 3, 3, 3], replicated, may hold values from -0.21875 to 0.21875
- bias_second: float32 [64], replicated, may hold values from -3 to 3
Outputs:
- grad_kernel_first: float32 [32, 4, 3, 3, 3], replicated
- grad_bias_first: float32 [32], replicated
- grad_kernel_second: float32 [64, 32, 3, 3, 3], replicated
- grad_bias_second: float32 [64], replicated
All inputs are finite; a program needn't handle non-finite values.
Results may differ from a plain program's by a relative error of at most 0.0031.
Values may be sent and summed in bfloat16 or wider, within the bound.
No kernel may reach another device: no remote copies, remote signals or barrier semaphores. Data moves between devices by JAX's collectives and lax.ppermute only.
A program may use at most 128 MiB of HBM per device.

v0:
```python
import jax
import jax.numpy as jnp
from jax import lax
from jax.sharding import PartitionSpec as P

GY = 8


def from_behind(value, axis, steps):
    count = lax.axis_size(axis)
    first, last = (max(0, -steps), min(count, count - steps))
    return lax.ppermute(value, axis, [(source, source + steps) for source in range(first, last)])


def correlate(padded, kernel):
    return lax.conv_general_dilated(
        padded,
        kernel,
        (1, 1, 1),
        "VALID",
        dimension_numbers=("NCDHW", "OIDHW", "NCDHW"),
        preferred_element_type=jnp.float32,
    )


def kernel_grad(padded, grads):
    result = lax.conv_general_dilated(
        padded,
        grads,
        (1, 1, 1),
        "VALID",
        dimension_numbers=("CNDHW", "IODHW", "NCDHW"),
        preferred_element_type=jnp.float32,
    )
    return jnp.transpose(result, (1, 0, 2, 3, 4))


def flipped(kernel):
    return jnp.transpose(kernel[:, :, ::-1, ::-1, ::-1], (1, 0, 2, 3, 4))


def spread_up(grad):
    batch, channels, rows_y, rows_z, rows_x = grad.shape
    value = grad.astype(jnp.float32) * 0.125
    value = jnp.broadcast_to(
        value[:, :, :, None, :, None, :, None], (batch, channels, rows_y, 2, rows_z, 2, rows_x, 2)
    )
    return value.reshape(batch, channels, 2 * rows_y, 2 * rows_z, 2 * rows_x)


def slope(pre):
    return jnp.where(pre > 0, 1.0, 0.3)


def bias_column(bias):
    return bias[None, :, None, None, None]


def widen_last(field):
    return jnp.pad(field, ((0, 0), (0, 0), (0, 0), (0, 0), (1, 1)))


def extend(field):
    grid_z = lax.axis_size("space") // GY
    place = lax.axis_index("space") % grid_z
    last_plane = field[:, :, :, -1:]
    first_plane = field[:, :, :, :1]
    last_plane = jnp.where(place < grid_z - 1, last_plane, jnp.zeros_like(last_plane))
    first_plane = jnp.where(place > 0, first_plane, jnp.zeros_like(first_plane))
    low_z = from_behind(last_plane, "space", 1)
    high_z = from_behind(first_plane, "space", -1)
    wide = jnp.concatenate([low_z, field, high_z], axis=3)
    low_y = from_behind(wide[:, :, -1:], "space", grid_z)
    high_y = from_behind(wide[:, :, :1], "space", -grid_z)
    return widen_last(jnp.concatenate([low_y, wide, high_y], axis=2))


def second_delta(second_ext, cotangent, kernel_second, bias_second):
    pre_two = correlate(second_ext, kernel_second) + bias_column(bias_second)
    return (spread_up(cotangent) * slope(pre_two)).astype(jnp.bfloat16)


def first_grads(first_ext, arrived, kernel_first, bias_first):
    pre_one = correlate(first_ext, kernel_first) + bias_column(bias_first)
    delta_one = (spread_up(arrived) * slope(pre_one)).astype(jnp.bfloat16)
    return (
        kernel_grad(first_ext, delta_one),
        jnp.sum(delta_one, axis=(0, 2, 3, 4), dtype=jnp.float32),
    )


def on_device(
    input_tiles, saved_tiles, out_grad_tiles, kernel_first, bias_first, kernel_second, bias_second
):
    first = input_tiles[0]
    second = saved_tiles[0]
    cotangent = out_grad_tiles[0]
    section = lax.axis_index("section")
    batches = first.shape[0]
    flipped_two = flipped(kernel_second)
    share = batches // lax.axis_size("section")
    offset = section * share
    local_first = lax.dynamic_slice_in_dim(first, offset, share, 0)
    local_second = lax.dynamic_slice_in_dim(second, offset, share, 0)
    local_cot = lax.dynamic_slice_in_dim(cotangent, offset, share, 0)
    second_ext = extend(local_second)
    first_ext = extend(local_first)
    delta_two = second_delta(second_ext, local_cot, kernel_second, bias_second)
    delta_ext = extend(delta_two)
    grad_w_two = kernel_grad(second_ext, delta_two)
    grad_b_two = jnp.sum(delta_two, axis=(0, 2, 3, 4), dtype=jnp.float32)
    back = correlate(delta_ext, flipped_two).astype(jnp.bfloat16)
    grad_w_one, grad_b_one = first_grads(first_ext, back, kernel_first, bias_first)
    total = lax.psum((grad_w_one, grad_b_one, grad_w_two, grad_b_two), ("section", "space"))
    return (total[0], total[1], total[2], total[3])


def solution(mesh):
    placed = (
        P("space", None, None, None, None, None),
        P("space", None, None, None, None, None),
        P("space", None, None, None, None, None),
        P(),
        P(),
        P(),
        P(),
    )
    return jax.shard_map(
        on_device, mesh=mesh, in_specs=placed, out_specs=(P(), P(), P(), P()), check_vma=False
    )
```

profile of v0, /device:TPU:0, one launch (start us, length us, event | category | flops | bytes accessed | tf_op | source)
XLA Modules:
  0.0 405.5 jit_solution(2935043332899590350)
XLA Ops:
  7.2 0.9 copy-done
  8.2 2.4 collective-permute-start
  10.7 1.3 collective-permute-start.1
  12.0 1.0 constant_dynamic-slice_fusion
  13.0 5.2 %collective-permute-start.4 = (bf16[1,32,4,1,128]{4,1,3,2,0:T(8,128)(2,1)S(1)}, bf16[1,32,4,1,128]{4,1,3,2,0:T(8,128)(2,1)S(1)}, u32[]{:S(2)}, u32[]{:S(2)}) collective-permute-start(bf16[1,32,4,1,128]{4,1,3,2,0:T(8,128)(2,1)S(1)} %get-tuple-element.19), channel_id=1, source_target_pairs={{0,1},{1,2},{2,3},{3,4},{4,5},{5,6},{6,7},{7,8},{8,9},{9,10},{10,1... | collective-permute-start | bytes 98312 | tf_op jit(solution)/shard_map/ppermute | solution.py:12
  18.1 1.3 collective-permute-start.5
  19.4 0.9 multiply_bitcast_fusion
  20.3 9.1 %copy.94 = bf16[1,4,8,8,256]{1,0,4,3,2:T(2,128)(2,1)} copy(bf16[1,4,8,8,256]{4,3,2,1,0:T(8,128)(2,1)S(1)} %dynamic-slice_bitcast_fusion) | data formatting | bytes 262144 | tf_op jit(solution)/shard_map/dynamic_slice | solution.py:103
  30.8 7.0 %pad_maximum_fusion.3 = (bf16[1,4,1,10,256]{1,0,4,3,2:T(2,128)(2,1)}, bf16[1,4,1,10,256]{1,0,4,3,2:T(2,128)(2,1)}) fusion(bf16[1,4,8,1,256]{1,0,4,3,2:T(2,128)(2,1)S(1)} %copy.95, bf16[1,4,8,8,256]{1,0,4,3,2:T(2,128)(2,1)} %copy.94, bf16[1,4,8,1,256]{1,0,4,3,2:T(2,128)(2,1)S(1)} %copy.93), kind=kLoop, calls=%fused_computation.43 | loop fusion | flops 40960 | bytes 204800 | tf_op jit(solution)/shard_map/slice | solution.py:73
  37.9 2.5 copy.96
  40.4 5.9 %collective-permute-start.2 = (bf16[1,4,1,10,256]{4,1,3,2,0:T(4,128)(2,1)S(1)}, bf16[1,4,1,10,256]{4,1,3,2,0:T(4,128)(2,1)S(1)}, u32[]{:S(2)}, u32[]{:S(2)}) collective-permute-start(bf16[1,4,1,10,256]{4,1,3,2,0:T(4,128)(2,1)S(1)} %copy.96), channel_id=1, source_target_pairs={{0,2},{1,3},{2,4},{3,5},{4,6},{5,7},{6,8},{7,9},{8,10},{9,11},{10,... | collective-permute-start | bytes 61448 | tf_op jit(solution)/shard_map/ppermute | solution.py:12
  46.3 2.5 copy.97
  48.8 1.3 collective-permute-start.3
  50.1 5.9 %collective-permute-start.6 = (bf16[1,32,1,6,128]{4,1,3,2,0:T(8,128)(2,1)S(1)}, bf16[1,32,1,6,128]{4,1,3,2,0:T(8,128)(2,1)S(1)}, u32[]{:S(2)}, u32[]{:S(2)}) collective-permute-start(bf16[1,32,1,6,128]{4,1,3,2,0:T(8,128)(2,1)S(1)} %get-tuple-element.17), channel_id=1, source_target_pairs={{0,2},{1,3},{2,4},{3,5},{4,6},{5,7},{6,8},{7,9},{8,10},{9,11},{10,... | collective-permute-start | bytes 147464 | tf_op jit(solution)/shard_map/ppermute | solution.py:12
  56.0 1.5 collective-permute-start.7
  57.5 2.2 copy.98
  59.7 2.2 copy.99
  61.8 40.1 %pad_maximum_fusion = bf16[1,4,10,10,256]{1,0,4,3,2:T(2,128)(2,1)} fusion(bf16[1,4,1,10,256]{1,0,4,3,2:T(2,128)(2,1)} %copy.99, bf16[1,4,8,1,256]{1,0,4,3,2:T(2,128)(2,1)S(1)} %copy.95, bf16[1,4,8,8,256]{1,0,4,3,2:T(2,128)(2,1)} %copy.94, bf16[1,4,8,1,256]{1,0,4,3,2:T(2,128)(2,1)S(1)} %copy.93, bf16[1,4,1,10,256]{1,0,4,3,2:T(2,128)(2,1)} %copy.98), kind=kLoop, calls=%fused_computation | loop fusion | flops 409600 | bytes 409600 | tf_op jit(solution)/shard_map/concatenate | solution.py:75
  101.9 23.7 %copy.113 = bf16[1,4,10,10,256]{4,1,3,2,0:T(4,128)(2,1)S(1)} copy(bf16[1,4,10,10,256]{1,0,4,3,2:T(2,128)(2,1)} %pad_maximum_fusion) | data formatting | bytes 409600 | tf_op jit(solution)/shard_map/concatenate | solution.py:75
  126.6 4.3 %copy.115 = bf16[4,10,10,1,8,33]{4,0,5,2,1,3:T(4,128)(2,1)} copy(bf16[4,10,10,1,8,33]{5,4,0,2,1,3:T(8,128)(2,1)S(1)} %reshape.57) | data formatting | bytes 422400 | tf_op jit(solution)/shard_map/conv_general_dilated | solution.py:16
  130.9 1.1 slice.64
  132.1 20.5 %fusion = f32[8,8,8,33,32]{4,2,3,1,0:T(8,128)S(1)} fusion(f32[32]{0:T(128)S(1)} %copy-done.9, pred[8,33]{0,1:T(8,128)(4,1)S(1)} %copy-done.11, bf16[32,4,3,3,3]{0,1,4,3,2:T(4,128)(2,1)S(1)} %copy-done.8, bf16[4,10,10,1,7,2]{4,0,5,2,1,3:T(4,128)(2,1)S(1)} %slice.64, bf16[4,10,10,1,8,33]{4,0,5,2,1,3:T(4,128)(2,1)} %copy.115), kind=kOutput, calls=%fused_computation.2 | convolution fusion | flops 119619840 | bytes 2392392 | tf_op jit(solution)/shard_map/conv_general_dilated | solution.py:16
  152.6 6.0 %copy.121 = f32[8,8,8,33,32]{4,3,2,1,0:T(8,128)} copy(f32[8,8,8,33,32]{4,2,3,1,0:T(8,128)S(1)} %fusion) | data formatting | bytes 4325376 | tf_op jit(solution)/shard_map/jit(_where)/select_n | solution.py:52
  158.6 9.5 %reshape.76 = f32[8,8,1,264,32]{4,3,1,0,2:T(8,128)} reshape(f32[8,8,8,33,32]{4,3,2,1,0:T(8,128)} %copy.121) | data formatting | bytes 4325376 | tf_op jit(solution)/shard_map/jit(_where)/select_n | solution.py:52
  169.0 1.7 reshape.45
  170.8 3.0 copy.103
  173.8 1.0 slice.58
  174.8 3.5 fusion.53
  178.9 1.1 convert_reduce_fusion.1
  180.0 1.4 broadcast_select_fusion.1
  181.6 2.0 collective-permute-start.8
  183.6 1.3 collective-permute-start.9
  184.9 0.8 pad_maximum_fusion.4
  185.7 4.7 %copy.119 = bf16[1,32,6,6,128]{1,0,4,3,2:T(2,128)(2,1)S(1)} copy(bf16[1,32,6,6,128]{4,1,3,2,0:T(8,128)(2,1)} %pad_maximum_fusion.4) | data formatting | bytes 589824 | tf_op jit(solution)/shard_map/concatenate | solution.py:75
  190.4 1.1 copy.105
  191.5 1.1 copy.107
  193.2 7.7 %collective-permute-start.10 = (bf16[1,64,1,6,128]{4,1,3,2,0:T(8,128)(2,1)}, bf16[1,64,1,6,128]{4,1,3,2,0:T(8,128)(2,1)S(1)}, u32[]{:S(2)}, u32[]{:S(2)}) collective-permute-start(bf16[1,64,1,6,128]{4,1,3,2,0:T(8,128)(2,1)} %get-tuple-element.15), channel_id=1, source_target_pairs={{0,2},{1,3},{2,4},{3,5},{4,6},{5,7},{6,8},{7,9},{8,10},{9,11},{10,... | collective-permute-start | bytes 294920 | tf_op jit(solution)/shard_map/ppermute | solution.py:12
  201.0 1.5 collective-permute-start.11
  202.4 14.7 %fusion.58 = f32[64,32,3,3,3]{0,1,4,3,2:T(8,128)} fusion(bf16[1,32,6,6,128]{1,0,4,3,2:T(2,128)(2,1)S(1)} %copy.119, bf16[1,64,4,4,128]{1,3,4,2,0:T(4,128)(2,1)S(1)} %get-tuple-element.8), kind=kOutput, calls=%fused_computation.50 | convolution fusion | flops 225312768 | bytes 778240 | tf_op jit(solution)/shard_map/transpose | solution.py:35
  217.2 1.0 maximum_bitcast_fusion
  218.2 0.7 copy.124
  220.0 0.7 copy-done.7
  220.7 4.3 %fusion.50 = f32[4,4,8,17,32]{4,2,3,1,0:T(8,128)S(1)} fusion(bf16[64,32,3,3,3]{0,1,4,3,2:T(8,128)(2,1)S(1)} %copy-done.7, bf16[64,6,6,1,7,2]{0,4,5,2,1,3:T(8,128)(2,1)S(1)} %slice.62, bf16[64,6,6,1,8,17]{0,4,5,2,1,3:T(8,128)(2,1)S(1)} %copy.110, pred[8,17]{0,1:T(8,128)(4,1)S(1)} %copy-done.12), kind=kOutput, calls=%fused_computation.40 | convolution fusion | flops 243027968 | bytes 1080456 | tf_op jit(solution)/shard_map/conv_general_dilated | solution.py:16
  225.6 7.3 %broadcast_in_dim.41 = f32[32,4,2,4,2,128,2]{0,6,5,4,3,2,1:T(2,128)} broadcast(f32[32,4,4,128]{0,3,2,1:T(8,128)S(1)} %copy.112), dimensions={0,1,3,5} | broadcast | bytes 2359296 | tf_op jit(solution)/shard_map/broadcast_in_dim | solution.py:45
  232.9 7.6 %convert_reduce_fusion = (f32[32]{0:T(128)}, bf16[1,32,8,8,256]{1,4,3,2,0:T(8,128)(2,1)S(1)}) fusion(f32[1,32,8,8,256]{1,4,3,2,0:T(8,128)} %bitcast.76, f32[8,8,1,264,32]{4,3,1,0,2:T(8,128)} %reshape.76), kind=kLoop, calls=%fused_computation.6 | loop fusion | flops 2097120 | bytes 5243008 | tf_op jit(solution)/shard_map/reduce_sum | solution.py:88
  240.5 111.0 %fusion.3 = f32[32,4,3,3,3]{0,1,4,3,2:T(4,128)S(1)} fusion(bf16[1,4,10,10,256]{1,0,4,3,2:T(2,128)(2,1)} %pad_maximum_fusion, bf16[1,32,8,8,256]{1,4,3,2,0:T(8,128)(2,1)S(1)} %get-tuple-element.10), kind=kOutput, calls=%fused_computation.7 | convolution fusion | flops 112951296 | bytes 1267200 | tf_op jit(solution)/shard_map/transpose | solution.py:35
  351.5 44.9 %all-reduce = (f32[32,4,3,3,3]{0,1,4,3,2:T(4,128)}, f32[32]{0:T(128)}, f32[64]{0:T(128)}) all-reduce(f32[32,4,3,3,3]{0,1,4,3,2:T(4,128)S(1)} %fusion.3, f32[32]{0:T(128)S(1)} %copy-done.4, f32[64]{0:T(128)S(1)} %copy-done.5), channel_id=1, replica_groups=mesh['section'=2,'space'=16] {'section','space'}, use_global_device_ids=true, to_apply=%region_0.1 | all-reduce | flops 3552 | bytes 28416 | tf_op jit(solution)/shard_map/psum | solution.py:114
  396.4 1.8 copy.132
  (64 shorter events, 6.5 us)
Async XLA Ops:
  7.2 1.0 copy-start
  7.2 389.2 %all-reduce.3.cloned.1.call-start = ((), (), s32[]{:S(2)}) async-start(), calls=%async_computation | async-start | bytes 884736 | tf_op jit(solution)/shard_map/psum | solution.py:114
  8.2 21.3 %collective-permute-start = (bf16[1,4,8,1,256]{4,2,3,1,0:T(8,128)(2,1)S(1)}, bf16[1,4,8,1,256]{4,2,3,1,0:T(8,128)(2,1)S(1)}, u32[]{:S(2)}, u32[]{:S(2)}) collective-permute-start(bf16[1,4,8,1,256]{4,2,3,1,0:T(8,128)(2,1)S(1)} %copy.91), channel_id=1, source_target_pairs={{0,1},{1,2},{2,3},{3,4},{4,5},{5,6},{6,7},{7,8},{8,9},{9,10},{10,1... | collective-permute-start | bytes 49160 | tf_op jit(solution)/shard_map/ppermute | solution.py:12
  10.7 19.5 %collective-permute-start.1 = (bf16[1,4,8,1,256]{4,2,3,1,0:T(8,128)(2,1)S(1)}, bf16[1,4,8,1,256]{4,2,3,1,0:T(8,128)(2,1)S(1)}, u32[]{:S(2)}, u32[]{:S(2)}) collective-permute-start(bf16[1,4,8,1,256]{4,2,3,1,0:T(8,128)(2,1)S(1)} %copy.92), channel_id=1, source_target_pairs={{1,0},{2,1},{3,2},{4,3},{5,4},{6,5},{7,6},{8,7},{9,8},{10,9},{11,1... | collective-permute-start | bytes 49160 | tf_op jit(solution)/shard_map/ppermute | solution.py:12
  13.0 37.1 %collective-permute-start.4 = (bf16[1,32,4,1,128]{4,1,3,2,0:T(8,128)(2,1)S(1)}, bf16[1,32,4,1,128]{4,1,3,2,0:T(8,128)(2,1)S(1)}, u32[]{:S(2)}, u32[]{:S(2)}) collective-permute-start(bf16[1,32,4,1,128]{4,1,3,2,0:T(8,128)(2,1)S(1)} %get-tuple-element.19), channel_id=1, source_target_pairs={{0,1},{1,2},{2,3},{3,4},{4,5},{5,6},{6,7},{7,8},{8,9},{9,10},{10,1... | collective-permute-start | bytes 98312 | tf_op jit(solution)/shard_map/ppermute | solution.py:12
  18.1 32.0 %collective-permute-start.5 = (bf16[1,32,4,1,128]{4,1,3,2,0:T(8,128)(2,1)S(1)}, bf16[1,32,4,1,128]{4,1,3,2,0:T(8,128)(2,1)S(1)}, u32[]{:S(2)}, u32[]{:S(2)}) collective-permute-start(bf16[1,32,4,1,128]{4,1,3,2,0:T(8,128)(2,1)S(1)} %get-tuple-element.20), channel_id=1, source_target_pairs={{1,0},{2,1},{3,2},{4,3},{5,4},{6,5},{7,6},{8,7},{9,8},{10,9},{11,1... | collective-permute-start | bytes 98312 | tf_op jit(solution)/shard_map/ppermute | solution.py:12
  40.4 17.1 %collective-permute-start.2 = (bf16[1,4,1,10,256]{4,1,3,2,0:T(4,128)(2,1)S(1)}, bf16[1,4,1,10,256]{4,1,3,2,0:T(4,128)(2,1)S(1)}, u32[]{:S(2)}, u32[]{:S(2)}) collective-permute-start(bf16[1,4,1,10,256]{4,1,3,2,0:T(4,128)(2,1)S(1)} %copy.96), channel_id=1, source_target_pairs={{0,2},{1,3},{2,4},{3,5},{4,6},{5,7},{6,8},{7,9},{8,10},{9,11},{10,... | collective-permute-start | bytes 61448 | tf_op jit(solution)/shard_map/ppermute | solution.py:12
  48.8 10.9 %collective-permute-start.3 = (bf16[1,4,1,10,256]{4,1,3,2,0:T(4,128)(2,1)S(1)}, bf16[1,4,1,10,256]{4,1,3,2,0:T(4,128)(2,1)S(1)}, u32[]{:S(2)}, u32[]{:S(2)}) collective-permute-start(bf16[1,4,1,10,256]{4,1,3,2,0:T(4,128)(2,1)S(1)} %copy.97), channel_id=1, source_target_pairs={{2,0},{3,1},{4,2},{5,3},{6,4},{7,5},{8,6},{9,7},{10,8},{11,9},{12,... | collective-permute-start | bytes 61448 | tf_op jit(solution)/shard_map/ppermute | solution.py:12
  50.1 118.0 %collective-permute-start.6 = (bf16[1,32,1,6,128]{4,1,3,2,0:T(8,128)(2,1)S(1)}, bf16[1,32,1,6,128]{4,1,3,2,0:T(8,128)(2,1)S(1)}, u32[]{:S(2)}, u32[]{:S(2)}) collective-permute-start(bf16[1,32,1,6,128]{4,1,3,2,0:T(8,128)(2,1)S(1)} %get-tuple-element.17), channel_id=1, source_target_pairs={{0,2},{1,3},{2,4},{3,5},{4,6},{5,7},{6,8},{7,9},{8,10},{9,11},{10,... | collective-permute-start | bytes 147464 | tf_op jit(solution)/shard_map/ppermute | solution.py:12
  56.0 112.2 %collective-permute-start.7 = (bf16[1,32,1,6,128]{4,1,3,2,0:T(8,128)(2,1)S(1)}, bf16[1,32,1,6,128]{4,1,3,2,0:T(8,128)(2,1)S(1)}, u32[]{:S(2)}, u32[]{:S(2)}) collective-permute-start(bf16[1,32,1,6,128]{4,1,3,2,0:T(8,128)(2,1)S(1)} %get-tuple-element.18), channel_id=1, source_target_pairs={{2,0},{3,1},{4,2},{5,3},{6,4},{7,5},{8,6},{9,7},{10,8},{11,9},{12,... | collective-permute-start | bytes 147464 | tf_op jit(solution)/shard_map/ppermute | solution.py:12
  126.6 5.5 %copy-start.8 = (bf16[32,4,3,3,3]{0,1,4,3,2:T(4,128)(2,1)S(1)}, bf16[32,4,3,3,3]{0,1,4,3,2:T(4,128)(2,1)}, u32[]{:S(2)}) copy-start(bf16[32,4,3,3,3]{0,1,4,3,2:T(4,128)(2,1)} %param.10) | copy-start | bytes 20740
  126.6 5.5 %copy-start.9 = (f32[32]{0:T(128)S(1)}, f32[32]{0:T(128)}, u32[]{:S(2)}) copy-start(f32[32]{0:T(128)} %param.11) | copy-start | bytes 388
  126.6 5.5 %copy-start.11 = (pred[8,33]{0,1:T(8,128)(4,1)S(1)}, pred[8,33]{0,1:T(8,128)(4,1)}, u32[]{:S(2)}) copy-start(pred[8,33]{0,1:T(8,128)(4,1)} %constant.64) | copy-start | bytes 796
  168.2 0.6 copy-start.2
  170.8 4.0 copy-start.6
  170.8 4.0 copy-start.10
  170.8 4.0 copy-start.12
  178.9 6.1 %copy-start.3 = (bf16[1,32,1,6,128]{4,1,3,2,0:T(8,128)(2,1)S(1)}, bf16[1,32,1,6,128]{4,1,3,2,0:T(8,128)(2,1)}, u32[]{:S(2)}) copy-start(bf16[1,32,1,6,128]{4,1,3,2,0:T(8,128)(2,1)} %copy-done.2) | copy-start | bytes 147460
  181.6 8.8 %collective-permute-start.8 = (bf16[1,64,4,1,128]{1,3,4,2,0:T(2,128)(2,1)}, bf16[1,64,4,1,128]{1,3,4,2,0:T(2,128)(2,1)}, u32[]{:S(2)}, u32[]{:S(2)}) collective-permute-start(bf16[1,64,4,1,128]{1,3,4,2,0:T(2,128)(2,1)} %get-tuple-element.13), channel_id=1, source_target_pairs={{0,1},{1,2},{2,3},{3,4},{4,5},{5,6},{6,7},{7,8},{8,9},{9,10},{10,1... | collective-permute-start | bytes 196616 | tf_op jit(solution)/shard_map/ppermute | solution.py:12
  183.6 7.8 %collective-permute-start.9 = (bf16[1,64,4,1,128]{1,3,4,2,0:T(2,128)(2,1)}, bf16[1,64,4,1,128]{1,3,4,2,0:T(2,128)(2,1)}, u32[]{:S(2)}, u32[]{:S(2)}) collective-permute-start(bf16[1,64,4,1,128]{1,3,4,2,0:T(2,128)(2,1)} %get-tuple-element.14), channel_id=1, source_target_pairs={{1,0},{2,1},{3,2},{4,3},{5,4},{6,5},{7,6},{8,7},{9,8},{10,9},{11,1... | collective-permute-start | bytes 196616 | tf_op jit(solution)/shard_map/ppermute | solution.py:12
  193.2 24.0 %collective-permute-start.10 = (bf16[1,64,1,6,128]{4,1,3,2,0:T(8,128)(2,1)}, bf16[1,64,1,6,128]{4,1,3,2,0:T(8,128)(2,1)S(1)}, u32[]{:S(2)}, u32[]{:S(2)}) collective-permute-start(bf16[1,64,1,6,128]{4,1,3,2,0:T(8,128)(2,1)} %get-tuple-element.15), channel_id=1, source_target_pairs={{0,2},{1,3},{2,4},{3,5},{4,6},{5,7},{6,8},{7,9},{8,10},{9,11},{10,... | collective-permute-start | bytes 294920 | tf_op jit(solution)/shard_map/ppermute | solution.py:12
  201.0 16.2 %collective-permute-start.11 = (bf16[1,64,1,6,128]{4,1,3,2,0:T(8,128)(2,1)S(1)}, bf16[1,64,1,6,128]{4,1,3,2,0:T(8,128)(2,1)}, u32[]{:S(2)}, u32[]{:S(2)}) collective-permute-start(bf16[1,64,1,6,128]{4,1,3,2,0:T(8,128)(2,1)S(1)} %get-tuple-element.16), channel_id=1, source_target_pairs={{2,0},{3,1},{4,2},{5,3},{6,4},{7,5},{8,6},{9,7},{10,8},{11,9},{12,... | collective-permute-start | bytes 294920 | tf_op jit(solution)/shard_map/ppermute | solution.py:12
  219.8 0.9 copy-start.7
  240.5 111.0 %copy-start.4 = (f32[32]{0:T(128)S(1)}, f32[32]{0:T(128)}, u32[]{:S(2)}) copy-start(f32[32]{0:T(128)} %get-tuple-element.9) | copy-start | bytes 388
  240.5 111.0 %copy-start.5 = (f32[64]{0:T(128)S(1)}, f32[64]{0:T(128)}, u32[]{:S(2)}) copy-start(f32[64]{0:T(128)} %get-tuple-element.7) | copy-start | bytes 772
  240.5 157.7 %copy-start.1 = (bf16[1,2,4,8,8,256]{5,4,3,2,1,0:T(8,128)(2,1)S(1)}, bf16[1,2,4,8,8,256]{5,4,3,2,1,0:T(8,128)(2,1)}, u32[]{:S(2)}) copy-start(bf16[1,2,4,8,8,256]{5,4,3,2,1,0:T(8,128)(2,1)} %param.7) | copy-start | bytes 786436
Sparse Core Ops, SparseCore 0:
  217.3 131.7 all-reduce.2
where the time goes:
time: 411 us; the launch traced here: 406 us
  matrix products  154 us (37%)
  local copies, waits for them, and re-layouts  93.5 us (23%)
  other arithmetic  60.7 us (15%)
  blocking collectives  44.9 us (11%)
  starting transfers between devices  37.2 us (9%)
  between operations  15.1 us (4%)
    transpose x2, matrix products, kernel_grad(): return jnp.transpose(result, (1, 0, 2, 3, 4))  126 us
    psum x1, blocking collectives, on_device(): lax.psum((grad_w_one, grad_b_one, grad_w_two, grad_b_two), ('section', 's...  44.9 us
    concatenate x4, other arithmetic, extend(): return widen_last(jnp.concatenate([low_y, wide, high_y], axis=2))  41.9 us
    ppermute x12, starting transfers between devices, from_behind(): lax.ppermute(value, axis, [(source, source + steps) for source in range(f...  37.2 us
    concatenate x5, local copies, waits for them, and re-layouts, extend(): return widen_last(jnp.concatenate([low_y, wide, high_y], axis=2))  29.2 us
    conv_general_dilated x3, matrix products, correlate(): lax.conv_general_dilated(padded, kernel, (1, 1, 1), 'VALID', dimension_nu...  28.4 us
    select_n x3, local copies, waits for them, and re-layouts, slope(): return jnp.where(pre > 0, 1.0, 0.3)  15.8 us
    conv_general_dilated x9, local copies, waits for them, and re-layouts, correlate(): lax.conv_general_dilated(padded, kernel, (1, 1, 1), 'VALID', dimension_nu...  12.5 us
  transfers between devices with their start and end apart: 13, of which 0 were waited for; matrix products, arithmetic and copies ran while one was open for 71% of the time, Pallas kernels for 0%

commit v1 on v0

v1 whole, which is shorter than its diff:
```python
import functools

import jax
import jax.numpy as jnp
import numpy as np
from jax import lax
from jax.experimental import pallas as pl
from jax.experimental.pallas import tpu as pltpu
from jax.sharding import PartitionSpec as P

GY = 8
BF = jnp.bfloat16
F32 = jnp.float32
LOW = np.float32(0.3) * np.float32(0.125)
SPAN = 48
ROWS = 512
VMEM = pl.BlockSpec(memory_space=pltpu.VMEM)


def pairs_of(count, stride, kind):
    size, cells = count
    out = []
    for i in range(size):
        p = (i // stride) % cells
        q = p ^ 1 if kind == 0 else (p + 1 if p % 2 else p - 1)
        if 0 <= q < cells:
            out.append((i, i + (q - p) * stride))
    return out


def first_tables():
    place = -np.ones((SPAN,), np.int64)
    chan = -np.ones((SPAN,), np.int64)
    for i in range(4):
        for z in range(8):
            place[i * 8 + z], chan[i * 8 + z] = z + 1, i
        place[32 + i], chan[32 + i] = 0, i
        place[36 + i], chan[36 + i] = 9, i
    pick = np.zeros((3, 112, 9 * SPAN), np.float32)
    fold = np.zeros((40, 9 * SPAN), np.float32)
    zext = np.full((9 * SPAN,), -100.0, np.float32)
    for a in range(3):
        for c in range(3):
            for r in range(SPAN):
                col = (a * 3 + c) * SPAN + r
                if chan[r] >= 0:
                    zext[col] = place[r]
                    fold[(a * 3 + c) * 4 + chan[r], col] = 1.0
                    for b in range(3):
                        pick[b, ((a * 3 + b) * 3 + c) * 4 + chan[r], col] = 1.0
    zrow = np.broadcast_to(zext[None, :], (8, 9 * SPAN)).copy()
    zcol = np.broadcast_to(zext[:, None], (9 * SPAN, 128)).copy()
    return pick, fold, zrow, zcol


def shifts(block):
    wide = block.astype(F32)
    size = wide.shape[1]
    lane = lax.broadcasted_iota(jnp.int32, wide.shape, 1)
    before = jnp.where(lane == 0, 0.0, pltpu.roll(wide, 1, 1)).astype(BF)
    after = jnp.where(lane == size - 1, 0.0, pltpu.roll(wide, size - 1, 1)).astype(BF)
    return before, block, after


def doubler(size):
    row = lax.broadcasted_iota(jnp.int32, (size, 2 * size), 0)
    col = lax.broadcasted_iota(jnp.int32, (size, 2 * size), 1)
    return jnp.where(lax.shift_right_logical(col, 1) == row, 1.0, 0.0).astype(BF)


def dot(a, b):
    return jnp.dot(a, b, preferred_element_type=F32)


def dot_nt(a, b):
    return lax.dot_general(a, b, (((1,), (1,)), ((), ())), preferred_element_type=F32)


def y_parity(grid_z):
    return lax.rem(lax.div(lax.axis_index("space"), grid_z), 2)


def z_parity(grid_z):
    return lax.rem(lax.rem(lax.axis_index("space"), grid_z), 2)


def y_pack(grid_z, x1_ref, g2_ref, x0_ref, a_ref, b_ref):
    mb = lax.axis_index("section")
    par = y_parity(grid_z)
    for ref, up in ((a_ref, 1 - par), (b_ref, par)):
        for p in range(2):
            for z in range(4):
                ref[(p * 4 + z) * 32 : (p * 4 + z + 1) * 32, :] = x1_ref[up * 2 + p, z]
        ref[256:320, :] = jnp.concatenate([g2_ref[up, 0], g2_ref[up, 1]], axis=1)
        for i in range(4):
            plane = x0_ref[0, mb, i, up * 7]
            ref[320 + i * 8 : 328 + i * 8, :] = plane[:, :128]
            ref[352 + i * 8 : 360 + i * 8, :] = plane[:, 128:]


def z_pack(grid_z, x1_ref, g2_ref, x0_ref, ra_ref, rb_ref, x1y_ref, g2y_ref, x0y_ref, *sends):
    mb = lax.axis_index("section")
    even = y_parity(grid_z) == 0
    ra = ra_ref[...]
    rb = rb_ref[...]
    low = jnp.where(even, rb, ra)
    high = jnp.where(even, ra, rb)
    for side, rim in ((0, low), (1, high)):
        for p in range(2):
            for z in range(4):
                x1y_ref[side * 6 + p, z] = rim[(p * 4 + z) * 32 : (p * 4 + z + 1) * 32]
        for z in range(2):
            g2y_ref[side * 3, z] = rim[256:320, z * 64 : z * 64 + 64]
        x0y_ref[:, side * 2304 : side * 2304 + 128] = rim[320:352]
        x0y_ref[:, side * 2304 + 128 : side * 2304 + 256] = rim[352:384]
    x1y_ref[2:6] = x1_ref[...]
    g2y_ref[1:3] = g2_ref[...]
    for i in range(4):
        for y in range(8):
            x0y_ref[i * 8 : i * 8 + 8, (1 + y) * 256 : (2 + y) * 256] = x0_ref[0, mb, i, y]
    zpar = z_parity(grid_z)
    for k in range(len(sends) // 3):
        sx1_ref, sg2_ref, sx0_ref = sends[3 * k : 3 * k + 3]
        up = 1 - zpar if k == 0 else zpar
        for y in range(8):
            for p in range(2):
                sx1_ref[y, p] = x1y_ref[y, up * 2 + p]
        for y in range(4):
            sg2_ref[y] = g2y_ref[y, up]
        row = lax.broadcasted_iota(jnp.int32, (16, 32), 0)
        col = lax.broadcasted_iota(jnp.int32, (16, 32), 1)
        take = jnp.where((col == row * 8 + up * 7) & (row < 4), 1.0, 0.0).astype(BF)
        sx0_ref[...] = dot(take, x0y_ref[...]).astype(BF)


def grads(grid_z, kinds, *refs):
    x1y_ref, g2y_ref, x0y_ref = refs[:3]
    got = refs[3 : 3 + 3 * kinds]
    w1_ref, b1_ref, w2_ref, b2_ref, pick_ref, fold_ref, zrow_ref, zcol_ref, out_ref = refs[
        3 + 3 * kinds : 12 + 3 * kinds
    ]
    xs, dz1, ds, x0s, dz0, up, wb0, w1f, w2d = refs[12 + 3 * kinds :]
    even = z_parity(grid_z) == 0

    def rims(which, index):
        one = got[which][index]
        two = got[3 + which][index] if kinds == 2 else jnp.zeros_like(one)
        return jnp.where(even, two, one), jnp.where(even, one, two)

    for y in range(8):
        rim = [rims(0, (y, p)) for p in range(2)]
        column = [rim[0][0], rim[1][0]] + [x1y_ref[y, z] for z in range(4)] + [rim[0][1], rim[1][1]]
        for z in range(8):
            for c, value in enumerate(shifts(column[z])):
                for a in range(3):
                    if 0 <= y - a < 6:
                        row = z * 288 + a * 96 + c * 32
                        xs[row : row + 32, (y - a) * 128 : (y - a + 1) * 128] = value

    w2 = w2_ref[...].astype(F32)
    w2 = jnp.concatenate(
        [w2[(a * 3 + b) * 96 : (a * 3 + b + 1) * 96] for b in range(3) for a in range(3)], axis=0
    )
    w2t = jnp.transpose(w2).astype(BF)
    for b in range(3):
        for a in range(3):
            for c in range(3):
                k = (2 - a) * 9 + (2 - b) * 3 + 2 - c
                at = (b * 9 + a * 3 + c) * 64
                w2d[:, at : at + 64] = w2_ref[k * 32 : k * 32 + 32]
    b2c = jnp.transpose(jnp.broadcast_to(b2_ref[...], (128, 64)))
    b1c = jnp.transpose(jnp.broadcast_to(b1_ref[...], (128, 32)))

    twice = doubler(64)
    coarse = []
    rim = [rims(1, (y,)) for y in range(4)]
    for z in range(4):
        plane = [
            rim[y][0] if z == 0 else rim[y][1] if z == 3 else g2y_ref[y, z - 1] for y in range(4)
        ]
        coarse.append(dot(jnp.concatenate(plane, axis=0), twice))
    for z in range(6):
        pre = dot(w2t, xs[z * 288 : z * 288 + 864, :])
        for y in range(6):
            at = (y + 1) // 2 * 64
            grad = coarse[(z + 1) // 2][at : at + 64]
            here = pre[:, y * 128 : y * 128 + 128] + b2c
            delta = (grad * jnp.where(here > 0, 0.125, LOW)).astype(BF)
            dz1[z * 64 : z * 64 + 64, y * 128 : y * 128 + 128] = delta
            for c, value in enumerate(shifts(delta)):
                for a in range(3):
                    if 0 <= y - a < 4:
                        row = z * 576 + a * 192 + c * 64
                        ds[row : row + 64, (y - a) * 128 : (y - a + 1) * 128] = value

    total = jnp.zeros((864, 64), F32)
    bias = jnp.zeros((8, 64), F32)
    ones = jnp.ones((8, 512), BF)
    for z in range(4):
        delta = dz1[(z + 1) * 64 : (z + 2) * 64, 128:640]
        total += dot_nt(xs[(z + 1) * 288 : (z + 1) * 288 + 864, 128:640], delta)
        bias += dot_nt(ones, delta)
    total = jnp.concatenate(
        [total[(b * 3 + a) * 96 : (b * 3 + a + 1) * 96] for a in range(3) for b in range(3)], axis=0
    )
    out_ref[:432, :64] = total[:432]
    out_ref[:432, 64:] = total[432:]
    out_ref[432:, :] = jnp.zeros((ROWS - 432, 128), F32)
    out_ref[472:480, :64] = bias

    back = [dot(w2d[...], ds[z * 576 : z * 576 + 1728, :]).astype(BF) for z in range(4)]
    stack = [back[z][:, y * 128 : y * 128 + 128] for y in range(4) for z in range(4)]
    up[...] = dot(jnp.concatenate(stack, axis=0), doubler(128))

    low, high = rims(2, Ellipsis)
    ones = jnp.where(lax.broadcasted_iota(jnp.int32, (8, 256), 0) == 0, 1.0, 0.0)
    for y in range(10):
        lanes = slice(y * 256, y * 256 + 256)
        block = jnp.concatenate(
            [
                x0y_ref[:, lanes].astype(F32),
                jnp.concatenate([low[:4, lanes].astype(F32), high[:4, lanes].astype(F32)], axis=0),
                ones,
            ],
            axis=0,
        ).astype(BF)
        for c, value in enumerate(shifts(block)):
            for a in range(3):
                if 0 <= y - a < 8:
                    row = (a * 3 + c) * SPAN
                    x0s[row : row + SPAN, (y - a) * 256 : (y - a + 1) * 256] = value

    w1f[108:112, :] = jnp.zeros((4, 32), F32)
    for k in range(27):
        w1f[k * 4 : k * 4 + 4, :] = w1_ref[k].astype(F32)
    w1t = jnp.transpose(w1f[...]).astype(BF)
    spread = [dot(w1t, pick_ref[b]) for b in range(3)]
    zrow = jnp.broadcast_to(zrow_ref[0:1, :], (32, 9 * SPAN))
    for z in range(8):
        value = jnp.zeros((32, 9 * SPAN), F32)
        for b in range(3):
            value = jnp.where(zrow == z + b, spread[b], value)
        wb0[z * 32 : z * 32 + 32, :] = value.astype(BF)

    b1w = jnp.concatenate([b1c, b1c], axis=1)
    for y in range(8):
        lanes = slice(y * 256, y * 256 + 256)
        pre = dot(wb0[...], x0s[:, lanes])
        for z in range(8):
            at = (y // 2) * 128 + (z // 2) * 32
            here = pre[z * 32 : z * 32 + 32] + b1w
            delta = up[at : at + 32, :] * jnp.where(here > 0, 0.125, LOW)
            dz0[z * 32 : z * 32 + 32, lanes] = delta.astype(BF)

    full = dot_nt(x0s[...], dz0[...])
    zcol = jnp.concatenate([zcol_ref[...], zcol_ref[...]], axis=1)
    zlane = lax.shift_right_logical(lax.broadcasted_iota(jnp.int32, full.shape, 1), 5).astype(F32)
    fold = fold_ref[...]
    for b in range(3):
        part = jnp.where(zcol == zlane + b, full, 0.0)
        part = lax.dot_general(
            fold,
            part,
            (((1,), (0,)), ((), ())),
            precision=lax.Precision.HIGHEST,
            preferred_element_type=F32,
        )
        part = sum(part[:, z * 32 : z * 32 + 32] for z in range(8))
        out_ref[432:472, b * 32 : b * 32 + 32] = part
    line = full[4 * SPAN + 40 : 4 * SPAN + 48]
    line = sum(line[:, z * 32 : z * 32 + 32] for z in range(8))
    out_ref[472:480, 64:96] = line


def unpack(sum_ref, g1_ref, b1_ref, g2_ref, b2_ref):
    g2_ref[:432, :] = sum_ref[:432, :64].astype(F32)
    g2_ref[432:, :] = sum_ref[:432, 64:].astype(F32)
    rest = sum_ref[432:480, :].astype(F32)
    for a in range(3):
        for b in range(3):
            for c in range(3):
                row = (a * 3 + c) * 4
                g1_ref[a * 9 + b * 3 + c] = rest[row : row + 4, b * 32 : b * 32 + 32]
    b2_ref[...] = rest[40:41, :64]
    b1_ref[...] = rest[40:41, 64:96]


def call(kernel, out, inputs, scratch=(), name=None):
    return pl.pallas_call(
        kernel,
        out_shape=out,
        in_specs=[VMEM] * len(inputs),
        out_specs=jax.tree.map(lambda _: VMEM, out),
        scratch_shapes=list(scratch),
        name=name,
    )(*inputs)


def shaped(*shape, dtype=BF):
    return jax.ShapeDtypeStruct(shape, dtype)


def on_device(grid_z, tables, x0, x1, g2, kernel_one, bias_one, kernel_two, bias_two):
    size = lax.axis_size("space")
    section = lax.axis_index("section")
    x1 = jnp.transpose(lax.dynamic_index_in_dim(x1[0], section, 0, False), (1, 2, 0, 3))
    g2 = jnp.transpose(lax.dynamic_index_in_dim(g2[0], section, 0, False), (1, 2, 0, 3))

    send = call(
        functools.partial(y_pack, grid_z), (shaped(384, 128),) * 2, (x1, g2, x0), name="y_pack"
    )
    got = [
        lax.ppermute(v, "space", pairs_of((size, GY), grid_z, k)) for k, v in enumerate(send)
    ]
    kinds = 1 if grid_z == 2 else 2
    sends = (shaped(8, 2, 32, 128), shaped(4, 64, 64), shaped(16, 2560)) * kinds
    wide = call(
        functools.partial(z_pack, grid_z),
        (shaped(8, 4, 32, 128), shaped(4, 2, 64, 64), shaped(32, 2560)) + sends,
        (x1, g2, x0, *got),
        name="z_pack",
    )
    rims = [
        lax.ppermute(v, "space", pairs_of((size, grid_z), 1, k // 3))
        for k, v in enumerate(wide[3:])
    ]
    w1 = jnp.transpose(kernel_one, (2, 3, 4, 1, 0)).reshape(27, 4, 32)
    w2 = jnp.transpose(kernel_two, (2, 3, 4, 1, 0)).reshape(864, 64)
    inputs = (*wide[:3], *rims, w1, bias_one[None], w2, bias_two[None], *tables)
    packed = call(
        functools.partial(grads, grid_z, kinds),
        shaped(ROWS, 128, dtype=F32),
        inputs,
        scratch=(
            pltpu.VMEM((2304, 768), BF),
            pltpu.VMEM((384, 768), BF),
            pltpu.VMEM((3456, 512), BF),
            pltpu.VMEM((9 * SPAN, 2048), BF),
            pltpu.VMEM((256, 2048), BF),
            pltpu.VMEM((512, 256), F32),
            pltpu.VMEM((256, 9 * SPAN), BF),
            pltpu.VMEM((112, 32), F32),
            pltpu.VMEM((32, 1728), BF),
        ),
        name="grads",
    )
    axes = ("section", "space")
    count = lax.axis_size(axes)
    parts = lax.all_to_all(packed, axes, 0, 0, tiled=True)
    mine = jnp.sum(parts.reshape(count, ROWS // count, 128), axis=0).astype(BF)
    mine = jnp.broadcast_to(mine[None], (count, ROWS // count, 128)).reshape(ROWS, 128)
    total = lax.all_to_all(mine, axes, 0, 0, tiled=True)
    g1, b1, g2, b2 = call(
        unpack,
        (
            shaped(27, 4, 32, dtype=F32),
            shaped(1, 32, dtype=F32),
            shaped(864, 64, dtype=F32),
            shaped(1, 64, dtype=F32),
        ),
        (total,),
        name="unpack",
    )
    g1 = jnp.transpose(g1.reshape(3, 3, 3, 4, 32), (4, 3, 0, 1, 2))
    g2 = jnp.transpose(g2.reshape(3, 3, 3, 32, 64), (4, 3, 0, 1, 2))
    return g1, b1[0], g2, b2[0]


def solution(mesh):
    pick, fold, zrow, zcol = first_tables()
    tables = (jnp.asarray(pick, BF), jnp.asarray(fold), jnp.asarray(zrow), jnp.asarray(zcol))
    grid_z = mesh.shape["space"] // GY
    placed = (P("space"),) * 3 + (P(),) * 4

    return jax.shard_map(
        functools.partial(on_device, grid_z, tables),
        mesh=mesh,
        in_specs=placed,
        out_specs=(P(),) * 4,
        check_vma=False,
    )
```

time: 411 us -> 57.9 us (0.14); the launches traced: 406 us -> 57.6 us
  matrix products: 154 us -> 0 us
  local copies, waits for them, and re-layouts: 93.5 us -> 4.25 us
  other arithmetic: 60.7 us -> 0.04 us
  starting transfers between devices: 37.2 us -> 4.2 us
  blocking collectives: 44.9 us -> 29.8 us
  Pallas kernels: 0 us -> 14.8 us
  between operations: 15.1 us -> 0.69 us
    transpose x2 -> x0, matrix products: 126 us -> none  [kernel_grad(): return jnp.transpose(result, (1, 0, 2, 3, 4))]
    psum x1 -> x0, blocking collectives: 44.9 us -> none  [on_device(): lax.psum((grad_w_one, grad_b_one, grad_w_two, grad_b_two), ('section', 's...]
    concatenate x4 -> x0, other arithmetic: 41.9 us -> none  [extend(): return widen_last(jnp.concatenate([low_y, wide, high_y], axis=2))]
    ppermute x12 -> x5, starting transfers between devices: 37.2 us -> 4.2 us  [the longest x2 3.65 us: on_device(): lax.ppermute(v, 'space', pairs_of((size, GY), grid_z, k))]
    all_to_all x0 -> x2, blocking collectives: none -> 29.8 us  [the longest x1 19.1 us: on_device(): parts = lax.all_to_all(packed, axes, 0, 0, tiled=True)]
    concatenate x5 -> x0, local copies, waits for them, and re-layouts: 29.2 us -> none  [extend(): return widen_last(jnp.concatenate([low_y, wide, high_y], axis=2))]
    conv_general_dilated x3 -> x0, matrix products: 28.4 us -> none  [correlate(): lax.conv_general_dilated(padded, kernel, (1, 1, 1), 'VALID', dimension_nu...]
    select_n x5 -> x0, local copies, waits for them, and re-layouts: 15.8 us -> none  [the longest x3 15.8 us: slope(): return jnp.where(pre > 0, 1.0, 0.3)]
  transfers between devices with their start and end apart: 13 -> 5, of which waited for: 0 -> 2; matrix products, arithmetic and copies ran while one was open for 71% -> 0% of each run, Pallas kernels for 0% -> 0%
where the time goes in v1:
time: 57.9 us; the launch traced here: 57.6 us
  blocking collectives  29.8 us (51%)
  Pallas kernels  14.8 us (26%)
  local copies, waits for them, and re-layouts  4.25 us (7%)
  starting transfers between devices  4.2 us (7%)
  waiting for transfers between devices  3.77 us (7%)
  between operations  0.69 us (1%)
    all_to_all x1, blocking collectives, on_device(): parts = lax.all_to_all(packed, axes, 0, 0, tiled=True)  19.1 us
    pallas_call x4, Pallas kernels, call(): pl.pallas_call(kernel, out_shape=out, in_specs=[VMEM] * len(inputs), out_...  14.8 us
    all_to_all x1, blocking collectives, on_device(): total = lax.all_to_all(mine, axes, 0, 0, tiled=True)  10.7 us
    ppermute x2, starting transfers between devices, on_device(): lax.ppermute(v, 'space', pairs_of((size, GY), grid_z, k))  3.65 us
    ppermute x2, waiting for transfers between devices, on_device(): lax.ppermute(v, 'space', pairs_of((size, GY), grid_z, k))  2.34 us
    unnamed x12, local copies, waits for them, and re-layouts  1.94 us
    dynamic_slice x2, local copies, waits for them, and re-layouts, on_device(): lax.dynamic_index_in_dim(g2[0], section, 0, False)  1.56 us
    ppermute x3, waiting for transfers between devices, on_device(): lax.ppermute(v, 'space', pairs_of((size, grid_z), 1, k // 3))  1.43 us
  transfers between devices with their start and end apart: 5, of which 2 were waited for; matrix products, arithmetic and copies ran while one was open for 0% of the time, Pallas kernels for 0%

profile of v1, /device:TPU:0, one launch (start us, length us, event | category | flops | bytes accessed | tf_op | source)
XLA Modules:
  0.0 57.6 jit_solution(4150221188692773735)
XLA Ops:
  0.6 0.0 copy-start
  0.7 0.9 %constant_dynamic-slice_fusion = bf16[1,1,64,2,2,64]{5,4,3,2,1,0:T(2,128)(2,1)S(1)} fusion(bf16[1,2,64,2,2,64]{5,4,3,2,1,0:T(2,128)(2,1)} %param.13, s32[]{:T(128)S(6)} %select_n.6), kind=kLoop, calls=%fused_computation.2 | loop fusion | bytes 65540 | tf_op jit(solution)/shard_map/jit(dynamic_index_in_dim)/dynamic_slice | solution.py:307
  1.6 0.6 %copy.20 = bf16[1,1,64,2,2,64]{5,2,4,3,1,0:T(8,128)(2,1)} copy(bf16[1,1,64,2,2,64]{5,4,3,2,1,0:T(2,128)(2,1)S(1)} %constant_dynamic-slice_fusion) | data formatting | bytes 65536 | tf_op jit(solution)/shard_map/jit(dynamic_index_in_dim)/dynamic_slice | solution.py:307
  2.2 0.0 copy-done
  2.3 0.7 %copy.19 = bf16[1,1,32,4,4,128]{5,2,4,3,1,0:T(8,128)(2,1)} copy(bf16[1,1,32,4,4,128]{5,4,3,2,1,0:T(4,128)(2,1)S(1)} %constant_dynamic-slice_fusion.1) | data formatting | bytes 262144 | tf_op jit(solution)/shard_map/jit(dynamic_index_in_dim)/dynamic_slice | solution.py:306
  2.9 1.8 %y_pack.1 = (bf16[384,128]{1,0:T(8,128)(2,1)}, bf16[384,128]{1,0:T(8,128)(2,1)}) custom-call(bf16[4,4,32,128]{3,2,1,0:T(8,128)(2,1)} %bitcast.28, bf16[2,2,64,64]{3,2,1,0:T(8,128)(2,1)} %bitcast.31, bf16[1,2,4,8,8,256]{5,4,3,2,1,0:T(8,128)(2,1)} %x0_ref.3), custom_call_target="tpu_custom_call" | custom-call | tf_op jit(solution)/shard_map/y_pack/pallas_call | solution.py:289
  4.7 3.0 %collective-permute-start = (bf16[384,128]{1,0:T(8,128)(2,1)}, bf16[384,128]{1,0:T(8,128)(2,1)S(1)}, u32[]{:S(2)}, u32[]{:S(2)}) collective-permute-start(bf16[384,128]{1,0:T(8,128)(2,1)} %get-tuple-element.16), channel_id=1, source_target_pairs={{0,2},{1,3},{2,0},{3,1},{4,6},{5,7},{6,4},{7,5},{8,10},{9,11},{10,... | collective-permute-start | bytes 294920 | tf_op jit(solution)/shard_map/ppermute | solution.py:313
  7.7 0.7 %collective-permute-start.1 = (bf16[384,128]{1,0:T(8,128)(2,1)}, bf16[384,128]{1,0:T(8,128)(2,1)S(1)}, u32[]{:S(2)}, u32[]{:S(2)}) collective-permute-start(bf16[384,128]{1,0:T(8,128)(2,1)} %get-tuple-element.17), channel_id=1, source_target_pairs={{2,4},{3,5},{4,2},{5,3},{6,8},{7,9},{8,6},{9,7},{10,12},{11,13},{1... | collective-permute-start | bytes 294920 | tf_op jit(solution)/shard_map/ppermute | solution.py:313
  8.4 2.3 %collective-permute-done.ra_ref = bf16[384,128]{1,0:T(8,128)(2,1)S(1)} collective-permute-done((bf16[384,128]{1,0:T(8,128)(2,1)}, bf16[384,128]{1,0:T(8,128)(2,1)S(1)}, u32[]{:S(2)}, u32[]{:S(2)}) %collective-permute-start) | collective-permute-done | bytes 98336 | tf_op jit(solution)/shard_map/ppermute | solution.py:313
  10.7 0.0 copy-start.2
  10.7 0.0 collective-permute-done.1.rb_ref
  10.7 0.6 %copy-done.2 = bf16[384,128]{1,0:T(8,128)(2,1)} copy-done((bf16[384,128]{1,0:T(8,128)(2,1)}, bf16[384,128]{1,0:T(8,128)(2,1)S(1)}, u32[]{:S(2)}) %copy-start.2) | copy-done | bytes 98328
  11.4 0.0 copy-start.3
  11.4 0.6 %copy-done.3 = bf16[384,128]{1,0:T(8,128)(2,1)} copy-done((bf16[384,128]{1,0:T(8,128)(2,1)}, bf16[384,128]{1,0:T(8,128)(2,1)S(1)}, u32[]{:S(2)}) %copy-start.3) | copy-done | bytes 98328
  12.0 2.1 %z_pack.1 = (bf16[8,4,32,128]{3,2,1,0:T(8,128)(2,1)}, bf16[4,2,64,64]{3,2,1,0:T(8,128)(2,1)}, bf16[32,2560]{1,0:T(8,128)(2,1)}, bf16[8,2,32,128]{3,2,1,0:T(8,128...) custom-call(bf16[4,4,32,128]{3,2,1,0:T(8,128)(2,1)} %bitcast.29, bf16[2,2,64,64]{3,2,1,0:T(8,128)(2,1)} %bitcast.32, ...), custom_call_target="tpu_custom_call" | custom-call | tf_op jit(solution)/shard_map/z_pack/pallas_call | solution.py:289
  14.1 0.0 collective-permute-start.2
  14.1 0.5 collective-permute-start.4
  14.6 0.0 collective-permute-start.3
  14.7 1.4 %collective-permute-done.3.refs_4_ = bf16[4,64,64]{2,1,0:T(8,128)(2,1)S(1)} collective-permute-done((bf16[4,64,64]{2,1,0:T(8,128)(2,1)}, bf16[4,64,64]{2,1,0:T(8,128)(2,1)S(1)}, u32[]{:S(2)}, u32[]{:S(2)}) %collective-permute-start.3) | collective-permute-done | bytes 32800 | tf_op jit(solution)/shard_map/ppermute | solution.py:324
  16.1 0.0 copy-start.5
  16.1 0.0 collective-permute-done.4.refs_5_
  16.1 0.0 copy-start.4
  16.1 0.0 collective-permute-done.2.refs_3_
  16.1 0.0 copy-start.1
  16.1 0.6 %copy-done.5 = bf16[4,64,64]{2,1,0:T(8,128)(2,1)} copy-done((bf16[4,64,64]{2,1,0:T(8,128)(2,1)}, bf16[4,64,64]{2,1,0:T(8,128)(2,1)S(1)}, u32[]{:S(2)}) %copy-start.5) | copy-done | bytes 32792
  16.7 0.0 copy-done.4
  16.7 0.1 copy-done.1
  16.8 9.1 %grads.1 = f32[512,128]{1,0:T(8,128)} custom-call(bf16[8,4,32,128]{3,2,1,0:T(8,128)(2,1)} %get-tuple-element.18.refs_0_, bf16[4,2,64,64]{3,2,1,0:T(8,128)(2,1)} %get-tuple-element.19.refs_1_, bf16[32,2560]{1,0:T(8,128)(2,1)} %get-tuple-element.20.refs_2_, bf16[8,2,32,128]{3,2,1,0:T(8,128)(2,1)} %copy-done.1, bf16[4,64,64]{2,1,0:T(8,128)(2,1)} %copy-done.5, ...), custom_call_target="tpu_custom_call" | custom-call | tf_op jit(solution)/shard_map/grads/pallas_call | solution.py:289
  25.9 19.1 %all_to_all.17 = f32[32,16,128]{2,1,0:T(8,128)S(1)} all-to-all(f32[32,16,128]{2,1,0:T(8,128)} %bitcast.30), channel_id=1, replica_groups=mesh['section'=2,'space'=16] {'section','space'}, dimensions={0} | all-to-all | bytes 524288 | tf_op jit(solution)/shard_map/all_to_all | solution.py:349
  45.1 10.7 %all_to_all.18 = bf16[32,16,128]{2,1,0:T(8,128)(2,1)} all-to-all(bf16[32,16,128]{2,1,0:T(8,128)(2,1)S(1)} %broadcast_in_dim.14), channel_id=1, replica_groups=mesh['section'=2,'space'=16] {'section','space'}, dimensions={0} | all-to-all | bytes 262144 | tf_op jit(solution)/shard_map/all_to_all | solution.py:352
  55.8 1.8 %unpack.1 = (f32[27,4,32]{2,1,0:T(4,128)}, f32[1,32]{1,0:T(1,128)}, f32[864,64]{1,0:T(8,128)}, f32[1,64]{1,0:T(1,128)}) custom-call(bf16[512,128]{1,0:T(8,128)(2,1)} %bitcast.33), custom_call_target="tpu_custom_call" | custom-call | tf_op jit(solution)/shard_map/unpack/pallas_call | solution.py:289
  (3 shorter events, 0.1 us)
Async XLA Ops:
  0.6 1.6 %copy-start = (bf16[1,2,32,4,4,128]{5,4,3,2,1,0:T(4,128)(2,1)S(1)}, bf16[1,2,32,4,4,128]{5,4,3,2,1,0:T(4,128)(2,1)}, u32[]{:S(2)}) copy-start(bf16[1,2,32,4,4,128]{5,4,3,2,1,0:T(4,128)(2,1)} %param.12) | copy-start | bytes 786436
  4.7 6.0 %collective-permute-start = (bf16[384,128]{1,0:T(8,128)(2,1)}, bf16[384,128]{1,0:T(8,128)(2,1)S(1)}, u32[]{:S(2)}, u32[]{:S(2)}) collective-permute-start(bf16[384,128]{1,0:T(8,128)(2,1)} %get-tuple-element.16), channel_id=1, source_target_pairs={{0,2},{1,3},{2,0},{3,1},{4,6},{5,7},{6,4},{7,5},{8,10},{9,11},{10,... | collective-permute-start | bytes 294920 | tf_op jit(solution)/shard_map/ppermute | solution.py:313
  7.7 3.0 %collective-permute-start.1 = (bf16[384,128]{1,0:T(8,128)(2,1)}, bf16[384,128]{1,0:T(8,128)(2,1)S(1)}, u32[]{:S(2)}, u32[]{:S(2)}) collective-permute-start(bf16[384,128]{1,0:T(8,128)(2,1)} %get-tuple-element.17), channel_id=1, source_target_pairs={{2,4},{3,5},{4,2},{5,3},{6,8},{7,9},{8,6},{9,7},{10,12},{11,13},{1... | collective-permute-start | bytes 294920 | tf_op jit(solution)/shard_map/ppermute | solution.py:313
  10.7 0.6 %copy-start.2 = (bf16[384,128]{1,0:T(8,128)(2,1)}, bf16[384,128]{1,0:T(8,128)(2,1)S(1)}, u32[]{:S(2)}) copy-start(bf16[384,128]{1,0:T(8,128)(2,1)S(1)} %collective-permute-done.ra_ref) | copy-start | bytes 294916
  11.4 0.6 %copy-start.3 = (bf16[384,128]{1,0:T(8,128)(2,1)}, bf16[384,128]{1,0:T(8,128)(2,1)S(1)}, u32[]{:S(2)}) copy-start(bf16[384,128]{1,0:T(8,128)(2,1)S(1)} %collective-permute-done.1.rb_ref) | copy-start | bytes 294916
  14.1 2.0 %collective-permute-start.2 = (bf16[8,2,32,128]{3,2,1,0:T(8,128)(2,1)}, bf16[8,2,32,128]{3,2,1,0:T(8,128)(2,1)S(1)}, u32[]{:S(2)}, u32[]{:S(2)}) collective-permute-start(bf16[8,2,32,128]{3,2,1,0:T(8,128)(2,1)} %get-tuple-element.21), channel_id=1, source_target_pairs={{0,1},{1,0},{2,3},{3,2},{4,5},{5,4},{6,7},{7,6},{8,9},{9,8},{10,11... | collective-permute-start | bytes 393224 | tf_op jit(solution)/shard_map/ppermute | solution.py:324
  14.1 2.0 %collective-permute-start.4 = (bf16[16,2560]{1,0:T(8,128)(2,1)}, bf16[16,2560]{1,0:T(8,128)(2,1)S(1)}, u32[]{:S(2)}, u32[]{:S(2)}) collective-permute-start(bf16[16,2560]{1,0:T(8,128)(2,1)} %get-tuple-element.23), channel_id=1, source_target_pairs={{0,1},{1,0},{2,3},{3,2},{4,5},{5,4},{6,7},{7,6},{8,9},{9,8},{10,11... | collective-permute-start | bytes 245768 | tf_op jit(solution)/shard_map/ppermute | solution.py:324
  14.6 1.5 %collective-permute-start.3 = (bf16[4,64,64]{2,1,0:T(8,128)(2,1)}, bf16[4,64,64]{2,1,0:T(8,128)(2,1)S(1)}, u32[]{:S(2)}, u32[]{:S(2)}) collective-permute-start(bf16[4,64,64]{2,1,0:T(8,128)(2,1)} %get-tuple-element.22), channel_id=1, source_target_pairs={{0,1},{1,0},{2,3},{3,2},{4,5},{5,4},{6,7},{7,6},{8,9},{9,8},{10,11... | collective-permute-start | bytes 98312 | tf_op jit(solution)/shard_map/ppermute | solution.py:324
  16.1 0.6 %copy-start.5 = (bf16[4,64,64]{2,1,0:T(8,128)(2,1)}, bf16[4,64,64]{2,1,0:T(8,128)(2,1)S(1)}, u32[]{:S(2)}) copy-start(bf16[4,64,64]{2,1,0:T(8,128)(2,1)S(1)} %collective-permute-done.3.refs_4_) | copy-start | bytes 98308
  16.1 0.6 %copy-start.4 = (bf16[16,2560]{1,0:T(8,128)(2,1)}, bf16[16,2560]{1,0:T(8,128)(2,1)S(1)}, u32[]{:S(2)}) copy-start(bf16[16,2560]{1,0:T(8,128)(2,1)S(1)} %collective-permute-done.4.refs_5_) | copy-start | bytes 245764
  16.1 0.7 %copy-start.1 = (bf16[8,2,32,128]{3,2,1,0:T(8,128)(2,1)}, bf16[8,2,32,128]{3,2,1,0:T(8,128)(2,1)S(1)}, u32[]{:S(2)}) copy-start(bf16[8,2,32,128]{3,2,1,0:T(8,128)(2,1)S(1)} %collective-permute-done.2.refs_3_) | copy-start | bytes 393220

commit v2 on v1

--- a/solution.py
+++ b/solution.py
@@ -285,13 +285,14 @@
     b1_ref[...] = rest[40:41, 64:96]
 
 
-def call(kernel, out, inputs, scratch=(), name=None):
+def call(kernel, out, inputs, scratch=(), name=None, room=8):
     return pl.pallas_call(
         kernel,
         out_shape=out,
         in_specs=[VMEM] * len(inputs),
         out_specs=jax.tree.map(lambda _: VMEM, out),
         scratch_shapes=list(scratch),
+        compiler_params=pltpu.CompilerParams(vmem_limit_bytes=room << 20),
         name=name,
     )(*inputs)
 
@@ -343,6 +344,7 @@
             pltpu.VMEM((32, 1728), BF),
         ),
         name="grads",
+        room=24,
     )
     axes = ("section", "space")
     count = lax.axis_size(axes)

time: 57.9 us -> 49.6 us (0.86)
  Pallas kernels: 14.8 us -> 8.07 us
  local copies, waits for them, and re-layouts: 4.25 us -> 2.54 us
  waiting for transfers between devices: 3.77 us -> 3.18 us
    pallas_call x4, Pallas kernels: 14.8 us -> 8.07 us  [call(): pl.pallas_call(kernel, out_shape=out, in_specs=[VMEM] * len(inputs), out_...]
    dynamic_slice x2, local copies, waits for them, and re-layouts: 0.72 us -> 0.09 us  [on_device(): lax.dynamic_index_in_dim(x1[0], section, 0, False)]
    dynamic_slice x2, local copies, waits for them, and re-layouts: 1.56 us -> 0.94 us  [on_device(): lax.dynamic_index_in_dim(g2[0], section, 0, False)]
    unnamed x12 -> x20, local copies, waits for them, and re-layouts: 1.94 us -> 1.48 us
where the time goes in v2:
time: 49.6 us; the launch traced here: 49.3 us
  blocking collectives  30.2 us (61%)
  Pallas kernels  8.07 us (16%)
  starting transfers between devices  4.49 us (9%)
  waiting for transfers between devices  3.18 us (6%)
  local copies, waits for them, and re-layouts  2.54 us (5%)
  between operations  0.78 us (2%)
    all_to_all x1, blocking collectives, on_device(): parts = lax.all_to_all(packed, axes, 0, 0, tiled=True)  19.7 us
    all_to_all x1, blocking collectives, on_device(): total = lax.all_to_all(mine, axes, 0, 0, tiled=True)  10.5 us
    pallas_call x4, Pallas kernels, call(): pl.pallas_call(kernel, out_shape=out, in_specs=[VMEM] * len(inputs), out_...  8.07 us
    ppermute x2, starting transfers between devices, on_device(): lax.ppermute(v, 'space', pairs_of((size, GY), grid_z, k))  3.85 us
    ppermute x2, waiting for transfers between devices, on_device(): lax.ppermute(v, 'space', pairs_of((size, GY), grid_z, k))  2 us
    unnamed x20, local copies, waits for them, and re-layouts  1.48 us
    ppermute x3, waiting for transfers between devices, on_device(): lax.ppermute(v, 'space', pairs_of((size, grid_z), 1, k // 3))  1.18 us
  transfers between devices with their start and end apart: 5, of which 2 were waited for; matrix products, arithmetic and copies ran while one was open for 0% of the time, Pallas kernels for 0%

profile of v2, /device:TPU:0, one launch (start us, length us, event | category | flops | bytes accessed | tf_op | source)
XLA Modules:
  0.0 49.3 jit_solution(13804016714127130312)
XLA Ops:
  0.6 0.0 copy-start
  0.7 0.9 %constant_dynamic-slice_fusion = bf16[1,1,64,2,2,64]{5,4,3,2,1,0:T(2,128)(2,1)S(1)} fusion(bf16[1,2,64,2,2,64]{5,4,3,2,1,0:T(2,128)(2,1)} %param.13, s32[]{:T(128)S(6)} %select_n.6), kind=kLoop, calls=%fused_computation.2 | loop fusion | bytes 65540 | tf_op jit(solution)/shard_map/jit(dynamic_index_in_dim)/dynamic_slice | solution.py:308
  1.6 0.0 copy-done
  1.6 0.0 copy-start.1
  1.6 0.1 constant_dynamic-slice_fusion.1
  1.7 0.8 %copy-done.1 = bf16[1,2,4,8,8,256]{5,4,3,2,1,0:T(8,128)(2,1)S(1)} copy-done((bf16[1,2,4,8,8,256]{5,4,3,2,1,0:T(8,128)(2,1)S(1)}, bf16[1,2,4,8,8,256]{5,4,3,2,1,0:T(8,128)(2,1)}, u32[]{:S(2)}) %copy-start.1) | copy-done | bytes 262168
  2.6 0.0 copy-start.4
  2.6 0.0 copy-start.7
  2.6 0.1 y_pack.1
  2.7 0.0 copy-start.2
  2.7 3.1 %collective-permute-start = (bf16[384,128]{1,0:T(8,128)(2,1)S(1)}, bf16[384,128]{1,0:T(8,128)(2,1)S(1)}, u32[]{:S(2)}, u32[]{:S(2)}) collective-permute-start(bf16[384,128]{1,0:T(8,128)(2,1)S(1)} %get-tuple-element.16), channel_id=1, source_target_pairs={{0,2},{1,3},{2,0},{3,1},{4,6},{5,7},{6,4},{7,5},{8,10},{9,11},{10,... | collective-permute-start | bytes 294920 | tf_op jit(solution)/shard_map/ppermute | solution.py:314
  5.7 0.0 copy-start.3
  5.7 0.0 copy-start.5
  5.7 0.8 %collective-permute-start.1 = (bf16[384,128]{1,0:T(8,128)(2,1)S(1)}, bf16[384,128]{1,0:T(8,128)(2,1)S(1)}, u32[]{:S(2)}, u32[]{:S(2)}) collective-permute-start(bf16[384,128]{1,0:T(8,128)(2,1)S(1)} %get-tuple-element.17), channel_id=1, source_target_pairs={{2,4},{3,5},{4,2},{5,3},{6,8},{7,9},{8,6},{9,7},{10,12},{11,13},{1... | collective-permute-start | bytes 294920 | tf_op jit(solution)/shard_map/ppermute | solution.py:314
  6.5 2.0 %collective-permute-done.ra_ref = bf16[384,128]{1,0:T(8,128)(2,1)S(1)} collective-permute-done((bf16[384,128]{1,0:T(8,128)(2,1)S(1)}, bf16[384,128]{1,0:T(8,128)(2,1)S(1)}, u32[]{:S(2)}, u32[]{:S(2)}) %collective-permute-start) | collective-permute-done | bytes 98336 | tf_op jit(solution)/shard_map/ppermute | solution.py:314
  8.5 0.0 collective-permute-done.1.rb_ref
  8.5 0.0 copy-start.6
  8.5 0.2 z_pack.1
  8.7 0.1 collective-permute-start.2
  8.8 0.5 %collective-permute-start.4 = (bf16[16,2560]{1,0:T(8,128)(2,1)S(1)}, bf16[16,2560]{1,0:T(8,128)(2,1)S(1)}, u32[]{:S(2)}, u32[]{:S(2)}) collective-permute-start(bf16[16,2560]{1,0:T(8,128)(2,1)S(1)} %get-tuple-element.23), channel_id=1, source_target_pairs={{0,1},{1,0},{2,3},{3,2},{4,5},{5,4},{6,7},{7,6},{8,9},{9,8},{10,11... | collective-permute-start | bytes 245768 | tf_op jit(solution)/shard_map/ppermute | solution.py:325
  9.3 0.1 collective-permute-start.3
  9.4 1.2 %collective-permute-done.3.refs_4_ = bf16[4,64,64]{2,1,0:T(8,128)(2,1)S(1)} collective-permute-done((bf16[4,64,64]{2,1,0:T(8,128)(2,1)S(1)}, bf16[4,64,64]{2,1,0:T(8,128)(2,1)S(1)}, u32[]{:S(2)}, u32[]{:S(2)}) %collective-permute-start.3) | collective-permute-done | bytes 32800 | tf_op jit(solution)/shard_map/ppermute | solution.py:325
  10.6 0.0 collective-permute-done.4.refs_5_
  10.6 0.0 collective-permute-done.2.refs_3_
  10.6 0.0 copy-start.8
  10.6 0.0 copy-start.9
  10.6 0.0 copy-done.4
  10.6 0.0 copy-done.7
  10.6 0.0 copy-done.2
  10.6 0.0 copy-done.3
  10.6 0.0 copy-done.5
  10.7 0.0 copy-done.6
  10.7 0.6 %copy-done.8 = f32[32]{0:T(128)S(1)} copy-done((f32[32]{0:T(128)S(1)}, f32[32]{0:T(128)}, u32[]{:S(2)}) %copy-start.8) | copy-done | bytes 152
  11.2 0.0 copy-done.9
  11.3 6.9 %grads.1 = f32[512,128]{1,0:T(8,128)S(1)} custom-call(bf16[8,4,32,128]{3,2,1,0:T(8,128)(2,1)S(1)} %get-tuple-element.18.refs_0_, bf16[4,2,64,64]{3,2,1,0:T(8,128)(2,1)S(1)} %get-tuple-element.19.refs_1_, bf16[32,2560]{1,0:T(8,128)(2,1)S(1)} %get-tuple-element.20.refs_2_, bf16[8,2,32,128]{3,2,1,0:T(8,128)(2,1)S(1)} %collective-permute-done.2.refs_3_, ...), custom_call_target="tpu_custom_call" | custom-call | tf_op jit(solution)/shard_map/grads/pallas_call | solution.py:289
  18.2 19.7 %all_to_all.17 = f32[32,16,128]{2,1,0:T(8,128)S(1)} all-to-all(f32[32,16,128]{2,1,0:T(8,128)S(1)} %bitcast.30), channel_id=1, replica_groups=mesh['section'=2,'space'=16] {'section','space'}, dimensions={0} | all-to-all | bytes 524288 | tf_op jit(solution)/shard_map/all_to_all | solution.py:351
  37.9 10.5 %all_to_all.18 = bf16[32,16,128]{2,1,0:T(8,128)(2,1)S(1)} all-to-all(bf16[32,16,128]{2,1,0:T(8,128)(2,1)S(1)} %broadcast_in_dim.14), channel_id=1, replica_groups=mesh['section'=2,'space'=16] {'section','space'}, dimensions={0} | all-to-all | bytes 262144 | tf_op jit(solution)/shard_map/all_to_all | solution.py:354
  48.5 0.9 %unpack.1 = (f32[27,4,32]{2,1,0:T(4,128)}, f32[1,32]{1,0:T(1,128)}, f32[864,64]{1,0:T(8,128)}, f32[1,64]{1,0:T(1,128)}) custom-call(bf16[512,128]{1,0:T(8,128)(2,1)S(1)} %bitcast.33), custom_call_target="tpu_custom_call" | custom-call | tf_op jit(solution)/shard_map/unpack/pallas_call | solution.py:289
  (4 shorter events, 0.1 us)
Async XLA Ops:
  0.6 1.0 %copy-start = (bf16[1,2,32,4,4,128]{5,4,3,2,1,0:T(4,128)(2,1)S(1)}, bf16[1,2,32,4,4,128]{5,4,3,2,1,0:T(4,128)(2,1)}, u32[]{:S(2)}) copy-start(bf16[1,2,32,4,4,128]{5,4,3,2,1,0:T(4,128)(2,1)} %param.12) | copy-start | bytes 786436
  1.6 0.9 %copy-start.1 = (bf16[1,2,4,8,8,256]{5,4,3,2,1,0:T(8,128)(2,1)S(1)}, bf16[1,2,4,8,8,256]{5,4,3,2,1,0:T(8,128)(2,1)}, u32[]{:S(2)}) copy-start(bf16[1,2,4,8,8,256]{5,4,3,2,1,0:T(8,128)(2,1)} %x0_ref.3) | copy-start | bytes 786436
  2.6 8.0 %copy-start.4 = (f32[432,128]{1,0:T(8,128)S(1)}, f32[432,128]{1,0:T(8,128)}, u32[]{:S(2)}) copy-start(f32[432,128]{1,0:T(8,128)} %constant.31.clone.refs_13_) | copy-start | bytes 663556
  2.6 8.0 %copy-start.7 = (f32[8,432]{1,0:T(8,128)S(1)}, f32[8,432]{1,0:T(8,128)}, u32[]{:S(2)}) copy-start(f32[8,432]{1,0:T(8,128)} %constant.30.clone.refs_12_) | copy-start | bytes 41476
  2.7 8.0 %copy-start.2 = (bf16[3,112,432]{2,1,0:T(8,128)(2,1)S(1)}, bf16[3,112,432]{2,1,0:T(8,128)(2,1)}, u32[]{:S(2)}) copy-start(bf16[3,112,432]{2,1,0:T(8,128)(2,1)} %constant.28.clone.refs_10_) | copy-start | bytes 870916
  2.7 5.9 %collective-permute-start = (bf16[384,128]{1,0:T(8,128)(2,1)S(1)}, bf16[384,128]{1,0:T(8,128)(2,1)S(1)}, u32[]{:S(2)}, u32[]{:S(2)}) collective-permute-start(bf16[384,128]{1,0:T(8,128)(2,1)S(1)} %get-tuple-element.16), channel_id=1, source_target_pairs={{0,2},{1,3},{2,0},{3,1},{4,6},{5,7},{6,4},{7,5},{8,10},{9,11},{10,... | collective-permute-start | bytes 294920 | tf_op jit(solution)/shard_map/ppermute | solution.py:314
  5.7 4.9 %copy-start.3 = (bf16[64,32,3,3,3]{0,1,4,3,2:T(8,128)(2,1)S(1)}, bf16[64,32,3,3,3]{0,1,4,3,2:T(8,128)(2,1)}, u32[]{:S(2)}) copy-start(bf16[64,32,3,3,3]{0,1,4,3,2:T(8,128)(2,1)} %param.16) | copy-start | bytes 331780
  5.7 4.9 %copy-start.5 = (f32[40,432]{1,0:T(8,128)S(1)}, f32[40,432]{1,0:T(8,128)}, u32[]{:S(2)}) copy-start(f32[40,432]{1,0:T(8,128)} %constant.29.clone.refs_11_) | copy-start | bytes 207364
  5.7 2.8 %collective-permute-start.1 = (bf16[384,128]{1,0:T(8,128)(2,1)S(1)}, bf16[384,128]{1,0:T(8,128)(2,1)S(1)}, u32[]{:S(2)}, u32[]{:S(2)}) collective-permute-start(bf16[384,128]{1,0:T(8,128)(2,1)S(1)} %get-tuple-element.17), channel_id=1, source_target_pairs={{2,4},{3,5},{4,2},{5,3},{6,8},{7,9},{8,6},{9,7},{10,12},{11,13},{1... | collective-permute-start | bytes 294920 | tf_op jit(solution)/shard_map/ppermute | solution.py:314
  8.5 2.1 %copy-start.6 = (bf16[32,4,3,3,3]{0,1,4,3,2:T(4,128)(2,1)S(1)}, bf16[32,4,3,3,3]{0,1,4,3,2:T(4,128)(2,1)}, u32[]{:S(2)}) copy-start(bf16[32,4,3,3,3]{0,1,4,3,2:T(4,128)(2,1)} %param.14) | copy-start | bytes 20740
  8.7 1.8 %collective-permute-start.2 = (bf16[8,2,32,128]{3,2,1,0:T(8,128)(2,1)S(1)}, bf16[8,2,32,128]{3,2,1,0:T(8,128)(2,1)S(1)}, u32[]{:S(2)}, u32[]{:S(2)}) collective-permute-start(bf16[8,2,32,128]{3,2,1,0:T(8,128)(2,1)S(1)} %get-tuple-element.21), channel_id=1, source_target_pairs={{0,1},{1,0},{2,3},{3,2},{4,5},{5,4},{6,7},{7,6},{8,9},{9,8},{10,11... | collective-permute-start | bytes 393224 | tf_op jit(solution)/shard_map/ppermute | solution.py:325
  8.8 1.8 %collective-permute-start.4 = (bf16[16,2560]{1,0:T(8,128)(2,1)S(1)}, bf16[16,2560]{1,0:T(8,128)(2,1)S(1)}, u32[]{:S(2)}, u32[]{:S(2)}) collective-permute-start(bf16[16,2560]{1,0:T(8,128)(2,1)S(1)} %get-tuple-element.23), channel_id=1, source_target_pairs={{0,1},{1,0},{2,3},{3,2},{4,5},{5,4},{6,7},{7,6},{8,9},{9,8},{10,11... | collective-permute-start | bytes 245768 | tf_op jit(solution)/shard_map/ppermute | solution.py:325
  9.3 1.3 %collective-permute-start.3 = (bf16[4,64,64]{2,1,0:T(8,128)(2,1)S(1)}, bf16[4,64,64]{2,1,0:T(8,128)(2,1)S(1)}, u32[]{:S(2)}, u32[]{:S(2)}) collective-permute-start(bf16[4,64,64]{2,1,0:T(8,128)(2,1)S(1)} %get-tuple-element.22), channel_id=1, source_target_pairs={{0,1},{1,0},{2,3},{3,2},{4,5},{5,4},{6,7},{7,6},{8,9},{9,8},{10,11... | collective-permute-start | bytes 98312 | tf_op jit(solution)/shard_map/ppermute | solution.py:325
  10.6 0.7 %copy-start.8 = (f32[32]{0:T(128)S(1)}, f32[32]{0:T(128)}, u32[]{:S(2)}) copy-start(f32[32]{0:T(128)} %param.15) | copy-start | bytes 388
  10.6 0.7 %copy-start.9 = (f32[64]{0:T(128)S(1)}, f32[64]{0:T(128)}, u32[]{:S(2)}) copy-start(f32[64]{0:T(128)} %param.17) | copy-start | bytes 772

commit v3 on v1

v3 whole, which is shorter than its diff:
```python
import functools

import jax
import jax.numpy as jnp
import numpy as np
from jax import lax
from jax.experimental import pallas as pl
from jax.experimental.pallas import tpu as pltpu
from jax.sharding import PartitionSpec as P

GY = 8
BF = jnp.bfloat16
F32 = jnp.float32
LOW = np.float32(0.3) * np.float32(0.125)
SPAN = 48
VMEM = pl.BlockSpec(memory_space=pltpu.VMEM)


def pairs_of(count, stride, kind):
    size, cells = count
    out = []
    for i in range(size):
        p = (i // stride) % cells
        q = p ^ 1 if kind == 0 else (p + 1 if p % 2 else p - 1)
        if 0 <= q < cells:
            out.append((i, i + (q - p) * stride))
    return out


def place_of(flat):
    block = lax.shift_right_logical(flat * 1366, 16)
    r = flat - block * SPAN
    chan = jnp.where(r < 32, lax.shift_right_logical(r, 3), r & 3)
    plane = jnp.where(r < 32, (r & 7) + 1, jnp.where(r < 36, 0, jnp.where(r < 40, 9, -100)))
    return block, chan, plane


def shifts(block):
    wide = block.astype(F32)
    size = wide.shape[1]
    lane = lax.broadcasted_iota(jnp.int32, wide.shape, 1)
    before = jnp.where(lane == 0, 0.0, pltpu.roll(wide, 1, 1)).astype(BF)
    after = jnp.where(lane == size - 1, 0.0, pltpu.roll(wide, size - 1, 1)).astype(BF)
    return before, block, after


def doubler(size):
    row = lax.broadcasted_iota(jnp.int32, (size, 2 * size), 0)
    col = lax.broadcasted_iota(jnp.int32, (size, 2 * size), 1)
    return jnp.where(lax.shift_right_logical(col, 1) == row, 1.0, 0.0).astype(BF)


def dot(a, b):
    return jnp.dot(a, b, preferred_element_type=F32)


def dot_nt(a, b):
    return lax.dot_general(a, b, (((1,), (1,)), ((), ())), preferred_element_type=F32)


def y_parity(grid_z):
    return lax.rem(lax.div(lax.axis_index("space"), grid_z), 2)


def z_parity(grid_z):
    return lax.rem(lax.rem(lax.axis_index("space"), grid_z), 2)


def y_pack(grid_z, x1_ref, g2_ref, x0_ref, a_ref, b_ref):
    par = y_parity(grid_z)
    for ref, up in ((a_ref, 1 - par), (b_ref, par)):
        for p in range(2):
            for z in range(4):
                ref[(p * 4 + z) * 32 : (p * 4 + z + 1) * 32, :] = x1_ref[up * 2 + p, z]
        ref[256:320, :] = jnp.concatenate([g2_ref[up, 0], g2_ref[up, 1]], axis=1)
        for i in range(4):
            plane = x0_ref[i, up * 7]
            ref[320 + i * 8 : 328 + i * 8, :] = plane[:, :128]
            ref[352 + i * 8 : 360 + i * 8, :] = plane[:, 128:]


def fetch(*refs):
    mb = lax.axis_index("section")
    sources, targets, sems = refs[:7], refs[7:14], refs[14]
    copies = [
        pltpu.make_async_copy(source.at[0, mb] if k < 3 else source, target, sems.at[k])
        for k, (source, target) in enumerate(zip(sources, targets))
    ]
    for copy in copies:
        copy.start()
    for copy in copies:
        copy.wait()


def z_pack(grid_z, ready_ref, x1_ref, g2_ref, x0_ref, ra_ref, rb_ref, x1r_ref, g2y_ref, x0r_ref, *sends):
    even = y_parity(grid_z) == 0
    ra = ra_ref[...]
    rb = rb_ref[...]
    low = jnp.where(even, rb, ra)
    high = jnp.where(even, ra, rb)
    for side, rim in ((0, low), (1, high)):
        for p in range(2):
            for z in range(4):
                x1r_ref[side * 2 + p, z] = rim[(p * 4 + z) * 32 : (p * 4 + z + 1) * 32]
        for z in range(2):
            g2y_ref[side * 3, z] = rim[256:320, z * 64 : z * 64 + 64]
        x0r_ref[side, :, :128] = rim[320:352]
        x0r_ref[side, :, 128:] = rim[352:384]
    g2y_ref[1:3] = g2_ref[...]
    zpar = z_parity(grid_z)
    for k in range(len(sends) // 3):
        sx1_ref, sg2_ref, sx0_ref = sends[3 * k : 3 * k + 3]
        up = 1 - zpar if k == 0 else zpar
        for y in range(8):
            for p in range(2):
                if 2 <= y < 6:
                    sx1_ref[y, p] = x1_ref[y - 2, up * 2 + p]
                else:
                    sx1_ref[y, p] = x1r_ref[y if y < 2 else y - 4, up * 2 + p]
        for y in range(4):
            sg2_ref[y] = g2y_ref[y, up]
        row = lax.broadcasted_iota(jnp.int32, (16, 32), 0)
        col = lax.broadcasted_iota(jnp.int32, (16, 32), 1)
        take = jnp.where((col == row * 8 + up * 7) & (row < 4), 1.0, 0.0).astype(BF)
        for y in range(10):
            if 1 <= y < 9:
                block = jnp.concatenate([x0_ref[i, y - 1] for i in range(4)], axis=0)
            else:
                block = x0r_ref[0 if y == 0 else 1]
            sx0_ref[:, y * 256 : y * 256 + 256] = dot(take, block).astype(BF)


def put_second(xs, y, z, block):
    for c, value in enumerate(shifts(block)):
        row = z * 96 + c * 32
        xs[row : row + 32, y * 128 : y * 128 + 128] = value


def put_first(x0s, y, start, block):
    for c, value in enumerate(shifts(block)):
        for a in range(3):
            if 0 <= y - a < 8:
                row = (a * 3 + c) * SPAN + start
                x0s[row : row + block.shape[0], (y - a) * 256 : (y - a + 1) * 256] = value


def prep(
    x1_ref, x0_ref, w1_ref, b1_ref, w2_ref, b2_ref,
    xs, x0s, wb2, wd, wb0, b1_out, b2_out, fold, zcol, w1f,
):
    for y in range(4):
        for z in range(4):
            put_second(xs, y + 2, z + 2, x1_ref[y, z])
    for y in range(8):
        block = jnp.concatenate([x0_ref[i, y] for i in range(4)], axis=0)
        put_first(x0s, y + 1, 0, block)
    wb2[...] = jnp.zeros_like(wb2)
    wd[...] = jnp.zeros_like(wd)
    for a in range(3):
        w2t = jnp.transpose(w2_ref[a * 288 : a * 288 + 288, :].astype(F32)).astype(BF)
        for z in range(6):
            wb2[a, z * 64 : z * 64 + 64, z * 96 : z * 96 + 288] = w2t
        for b in range(3):
            for c in range(3):
                k = (2 - a) * 9 + (2 - b) * 3 + 2 - c
                value = w2_ref[k * 32 : k * 32 + 32]
                for z in range(4):
                    at = (z + b) * 192 + c * 64
                    wd[a, z * 32 : z * 32 + 32, at : at + 64] = value
    b2_out[...] = jnp.transpose(jnp.broadcast_to(b2_ref[...], (128, 64)))
    b1_out[...] = jnp.transpose(jnp.broadcast_to(b1_ref[...], (128, 32)))
    block, chan, plane = place_of(lax.broadcasted_iota(jnp.int32, fold.shape, 1))
    row = lax.broadcasted_iota(jnp.int32, fold.shape, 0)
    fold[...] = jnp.where((row == block * 4 + chan) & (plane >= 0), 1.0, 0.0)
    zcol[...] = place_of(lax.broadcasted_iota(jnp.int32, zcol.shape, 0))[2].astype(F32)
    w1f[108:112, :] = jnp.zeros((4, 32), F32)
    for k in range(27):
        w1f[k * 4 : k * 4 + 4, :] = w1_ref[k].astype(F32)
    w1t = jnp.transpose(w1f[...]).astype(BF)
    block, chan, plane = place_of(lax.broadcasted_iota(jnp.int32, (112, 9 * SPAN), 1))
    row = lax.broadcasted_iota(jnp.int32, (112, 9 * SPAN), 0)
    third = lax.shift_right_logical(block * 11, 5)
    home = jnp.where(plane >= 0, third * 24 + block * 4 + chan, -100)
    spread = [dot(w1t, jnp.where(row == home + b * 12, 1.0, 0.0).astype(BF)) for b in range(3)]
    zrow = place_of(lax.broadcasted_iota(jnp.int32, (32, 9 * SPAN), 1))[2]
    for z in range(8):
        value = jnp.zeros((32, 9 * SPAN), F32)
        for b in range(3):
            value = jnp.where(zrow == z + b, spread[b], value)
        wb0[z * 32 : z * 32 + 32, :] = value.astype(BF)


def rims_in(xs_in, x0s_in, x1r_ref, x0r_ref, xs, x0s):
    for k, y in enumerate((0, 1, 6, 7)):
        for z in range(4):
            put_second(xs, y, z + 2, x1r_ref[k, z])
    for k, y in enumerate((0, 9)):
        put_first(x0s, y, 0, x0r_ref[k])


def rims_of(grid_z, kinds, got):
    even = z_parity(grid_z) == 0

    def rims(ref, index):
        one = got[ref][index]
        two = got[len(got) // 2 + ref][index] if kinds == 2 else jnp.zeros_like(one)
        return jnp.where(even, two, one), jnp.where(even, one, two)

    return rims


def second_grads(grid_z, kinds, *refs):
    xs_in, wb2, b2_ref, g2y_ref = refs[:4]
    rims = rims_of(grid_z, kinds, refs[4 : 4 + 3 * kinds])
    xs, ds, keep_ref, send_ref, bias_ref, dz1 = refs[4 + 3 * kinds :]

    for y in range(8):
        for p in range(2):
            low, high = rims(0, (y, p))
            put_second(xs, y, p, low)
            put_second(xs, y, 6 + p, high)

    twice = doubler(64)
    coarse = []
    rim = [rims(1, (y,)) for y in range(4)]
    for z in range(4):
        plane = [
            rim[y][0] if z == 0 else rim[y][1] if z == 3 else g2y_ref[y, z - 1] for y in range(4)
        ]
        coarse.append(dot(jnp.concatenate(plane, axis=0), twice))
    b2c = b2_ref[...]
    for half in range(3):
        pre = dot(wb2[0], xs[:, half * 256 : half * 256 + 256])
        pre += dot(wb2[1], xs[:, half * 256 + 128 : half * 256 + 384])
        pre += dot(wb2[2], xs[:, half * 256 + 256 : half * 256 + 512])
        for y in (2 * half, 2 * half + 1):
            at = (y + 1) // 2 * 64
            for z in range(6):
                grad = coarse[(z + 1) // 2][at : at + 64]
                here = pre[z * 64 : z * 64 + 64, (y % 2) * 128 : (y % 2) * 128 + 128] + b2c
                delta = (grad * jnp.where(here > 0, 0.125, LOW)).astype(BF)
                dz1[z * 64 : z * 64 + 64, y * 128 : y * 128 + 128] = delta
                for c, value in enumerate(shifts(delta)):
                    row = z * 192 + c * 64
                    ds[row : row + 64, y * 128 : y * 128 + 128] = value

    own = dz1[64:320, 128:640]
    line = dot_nt(jnp.ones((8, 512), BF), own)
    bias_ref[...] = sum(line[:, z * 64 : z * 64 + 64] for z in range(4))
    parts = []
    for a in range(3):
        full = dot_nt(xs[96:672, (a + 1) * 128 : (a + 5) * 128], own)
        parts.append(sum(full[z * 96 : z * 96 + 288, z * 64 : z * 64 + 64] for z in range(4)))
    even = z_parity(grid_z) == 0
    low = (parts[0][:216], jnp.concatenate([parts[0][216:], parts[1][:144]], axis=0))
    high = (jnp.concatenate([parts[1][144:], parts[2][:72]], axis=0), parts[2][72:])
    for k in range(2):
        keep_ref[:216, k * 64 : k * 64 + 64] = jnp.where(even, low[k], high[k])
        send_ref[:, k * 64 : k * 64 + 64] = jnp.where(even, high[k], low[k])


def first_grads(grid_z, kinds, *refs):
    x0s_in, ds, wd, wb0, b1_ref, fold_ref, zcol_ref = refs[:7]
    rims = rims_of(grid_z, kinds, refs[7 : 7 + kinds])
    x0s, out_ref, line_ref, dz0, up = refs[7 + kinds :]

    back = dot(wd[0], ds[:, :512])
    back += dot(wd[1], ds[:, 128:640])
    back += dot(wd[2], ds[:, 256:768])
    back = back.astype(BF)
    stack = [back[:, y * 128 : y * 128 + 128] for y in range(4)]
    up[...] = dot(jnp.concatenate(stack, axis=0), doubler(128))

    low, high = rims(0, Ellipsis)
    ones = jnp.where(lax.broadcasted_iota(jnp.int32, (8, 256), 0) == 0, 1.0, 0.0)
    for y in range(10):
        lanes = slice(y * 256, y * 256 + 256)
        pair = jnp.concatenate([low[:4, lanes].astype(F32), high[:4, lanes].astype(F32)], axis=0)
        put_first(x0s, y, 32, jnp.concatenate([pair, ones], axis=0).astype(BF))

    b1w = jnp.concatenate([b1_ref[...], b1_ref[...]], axis=1)
    for y in range(8):
        lanes = slice(y * 256, y * 256 + 256)
        pre = dot(wb0[...], x0s[:, lanes])
        for z in range(8):
            at = (y // 2) * 128 + (z // 2) * 32
            here = pre[z * 32 : z * 32 + 32] + b1w
            delta = up[at : at + 32, :] * jnp.where(here > 0, 0.125, LOW)
            dz0[z * 32 : z * 32 + 32, lanes] = delta.astype(BF)

    full = dot_nt(x0s[...], dz0[...])
    zcol = zcol_ref[...]
    lane = lax.broadcasted_iota(jnp.int32, zcol.shape, 1)
    zlane = lax.shift_right_logical(lane, 5).astype(F32)
    every = []
    for b in range(3):
        part = jnp.where(zcol == zlane + b, full[:, :128], 0.0)
        part += jnp.where(zcol == zlane + (b + 4), full[:, 128:], 0.0)
        part += pltpu.roll(part, 64, 1)
        every.append(part + pltpu.roll(part, 32, 1))
    part = jnp.where(lane < 32, every[0], jnp.where(lane < 64, every[1], every[2]))
    part = lax.dot_general(
        fold_ref[...],
        part,
        (((1,), (0,)), ((), ())),
        precision=lax.Precision.HIGHEST,
        preferred_element_type=F32,
    )
    out_ref[...] = part
    line = full[4 * SPAN + 40 : 4 * SPAN + 48]
    line_ref[...] = sum(line[:, z * 32 : z * 32 + 32] for z in range(8))


def pack_grads(count, deep, keep_ref, got_ref, bias_two_ref, part_ref, bias_one_ref, out_ref, flat):
    flat[...] = jnp.zeros_like(flat)
    flat[:216, :] = keep_ref[...] + got_ref[...]
    at = (deep - 1) * count
    flat[at : at + 27, :96] = part_ref[:27, :96]
    for b in range(3):
        flat[at + b * 9 : at + b * 9 + 9, 96:] = part_ref[27:36, b * 32 : b * 32 + 32]
    flat[at + 27 : at + 28, :64] = bias_two_ref[:1, :]
    flat[at + 27 : at + 28, 64:96] = bias_one_ref[:1, :]
    for k in range(deep):
        out_ref[:, k, :] = flat[k * count : (k + 1) * count, :]


def sum_parts(count, deep, parts_ref, out_ref):
    sums = [parts_ref[0], parts_ref[1]]
    for k in range(1, count // 2):
        sums[0] += parts_ref[2 * k]
        sums[1] += parts_ref[2 * k + 1]
    row = lax.broadcasted_iota(jnp.int32, (deep, 128), 0)
    sums[0] += jnp.where(row == deep - 1, sums[1], 0.0)
    for k in range(count):
        out_ref[k, 0] = sums[0].astype(BF)
        out_ref[k, 1] = sums[1].astype(BF)


def unpack(count, deep, sum_ref, g1_ref, b1_ref, g2_ref, b2_ref, flat):
    for half in range(2):
        for k in range(deep - 1):
            flat[k * count : (k + 1) * count, :] = sum_ref[:, half, k, :].astype(F32)
        g2_ref[half * 432 : half * 432 + 216, :] = flat[:216, :64]
        g2_ref[half * 432 + 216 : half * 432 + 432, :] = flat[:216, 64:]
    flat[:count, :] = sum_ref[:, 0, deep - 1, :].astype(F32)
    for a in range(3):
        for b in range(3):
            for c in range(3):
                row = (a * 3 + c) * 4
                for i in range(4):
                    r = row + i
                    if r < 27:
                        value = flat[r : r + 1, b * 32 : b * 32 + 32]
                    else:
                        value = flat[b * 9 + r - 27 : b * 9 + r - 26, 96:]
                    g1_ref[a * 9 + b * 3 + c, i : i + 1] = value
    b2_ref[...] = flat[27:28, :64]
    b1_ref[...] = flat[27:28, 64:96]


def call(kernel, out, inputs, scratch=(), name=None, room=8, specs=None, alias=None):
    return pl.pallas_call(
        kernel,
        out_shape=out,
        in_specs=specs or [VMEM] * len(inputs),
        out_specs=jax.tree.map(lambda _: VMEM, out),
        scratch_shapes=list(scratch),
        input_output_aliases=alias or {},
        name=name,
        compiler_params=pltpu.CompilerParams(vmem_limit_bytes=room << 20),
    )(*inputs)


def shaped(*shape, dtype=BF):
    return jax.ShapeDtypeStruct(shape, dtype)


def on_device(grid_z, x0, x1, g2, kernel_one, bias_one, kernel_two, bias_two):
    size = lax.axis_size("space")
    w1 = jnp.transpose(kernel_one, (2, 3, 4, 1, 0)).reshape(27, 4, 32)
    w2 = jnp.transpose(kernel_two, (2, 3, 4, 1, 0)).reshape(864, 64)
    inputs = (x0, x1, g2, w1, bias_one[None], w2, bias_two[None])
    x0, x1, g2, w1, b1, w2, b2 = call(
        fetch,
        (
            shaped(4, 8, 8, 256),
            shaped(32, 4, 4, 128),
            shaped(64, 2, 2, 64),
            shaped(27, 4, 32),
            shaped(1, 32, dtype=F32),
            shaped(864, 64),
            shaped(1, 64, dtype=F32),
        ),
        tuple(pltpu.with_memory_space_constraint(v, pltpu.HBM) for v in inputs),
        scratch=(pltpu.SemaphoreType.DMA((7,)),),
        specs=[pl.BlockSpec(memory_space=pltpu.HBM)] * 7,
        name="fetch",
    )
    x1 = jnp.transpose(x1, (1, 2, 0, 3))
    g2 = jnp.transpose(g2, (1, 2, 0, 3))

    send = call(
        functools.partial(y_pack, grid_z), (shaped(384, 128),) * 2, (x1, g2, x0), name="y_pack"
    )
    got = [lax.ppermute(v, "space", pairs_of((size, GY), grid_z, k)) for k, v in enumerate(send)]
    xs, x0s, wb2, wd, wb0, b1, b2, fold, zcol = call(
        prep,
        (
            shaped(768, 1024),
            shaped(9 * SPAN, 2048),
            shaped(3, 384, 768),
            shaped(3, 128, 1152),
            shaped(256, 9 * SPAN),
            shaped(32, 128, dtype=F32),
            shaped(64, 128, dtype=F32),
            shaped(40, 9 * SPAN, dtype=F32),
            shaped(9 * SPAN, 128, dtype=F32),
        ),
        (x1, x0, w1, b1, w2, b2),
        scratch=(pltpu.VMEM((112, 32), F32),),
        name="prep",
    )
    kinds = 1 if grid_z == 2 else 2
    sends = (shaped(8, 2, 32, 128), shaped(4, 64, 64), shaped(16, 2560)) * kinds
    wide = call(
        functools.partial(z_pack, grid_z),
        (shaped(4, 4, 32, 128), shaped(4, 2, 64, 64), shaped(2, 32, 256)) + sends,
        (b1, x1, g2, x0, *got),
        name="z_pack",
    )
    rims = [
        lax.ppermute(v, "space", pairs_of((size, grid_z), 1, k // 3))
        for k, v in enumerate(wide[3:])
    ]
    xs, x0s = call(
        rims_in,
        (shaped(768, 1024), shaped(9 * SPAN, 2048)),
        (xs, x0s, wide[0], wide[2]),
        alias={0: 0, 1: 1},
        name="rims_in",
    )
    xs, ds, keep, swap, line_two = call(
        functools.partial(second_grads, grid_z, kinds),
        (
            shaped(768, 1024),
            shaped(1152, 768),
            shaped(216, 128, dtype=F32),
            shaped(216, 128, dtype=F32),
            shaped(8, 64, dtype=F32),
        ),
        (xs, wb2, b2, wide[1], *rims),
        scratch=(pltpu.VMEM((384, 768), BF),),
        alias={0: 0},
        name="second_grads",
    )
    swap = lax.ppermute(swap, "space", [(k, k ^ 1) for k in range(size)])
    x0s, part_one, line_one = call(
        functools.partial(first_grads, grid_z, kinds),
        (shaped(9 * SPAN, 2048), shaped(40, 128, dtype=F32), shaped(8, 32, dtype=F32)),
        (x0s, ds, wd, wb0, b1, fold, zcol, *rims[2::3]),
        scratch=(pltpu.VMEM((256, 2048), BF), pltpu.VMEM((512, 256), F32)),
        alias={0: 0},
        name="first_grads",
    )
    axes = ("section", "space")
    count = lax.axis_size(axes)
    deep = -(-216 // count) + 1
    shape = shaped(count, deep, 128, dtype=F32)
    lines = (pltpu.VMEM((deep * count, 128), F32),)
    packed = call(
        functools.partial(pack_grads, count, deep),
        shape,
        (keep, swap, line_two, part_one, line_one),
        scratch=lines,
        name="pack_grads",
    )
    parts = lax.all_to_all(packed, axes, 0, 0, tiled=True)
    mine = call(
        functools.partial(sum_parts, count, deep),
        shaped(count, 2, deep, 128),
        (parts,),
        name="sum_parts",
    )
    total = lax.all_to_all(mine, axes, 0, 0, tiled=True)
    g1, b1, g2, b2 = call(
        functools.partial(unpack, count, deep),
        (
            shaped(27, 4, 32, dtype=F32),
            shaped(1, 32, dtype=F32),
            shaped(864, 64, dtype=F32),
            shaped(1, 64, dtype=F32),
        ),
        (total,),
        scratch=lines,
        name="unpack",
    )
    g1 = jnp.transpose(g1.reshape(3, 3, 3, 4, 32), (4, 3, 0, 1, 2))
    g2 = jnp.transpose(g2.reshape(3, 3, 3, 32, 64), (4, 3, 0, 1, 2))
    return g1, b1[0], g2, b2[0]


def solution(mesh):
    grid_z = mesh.shape["space"] // GY
    placed = (P("space"),) * 3 + (P(),) * 4

    return jax.shard_map(
        functools.partial(on_device, grid_z),
        mesh=mesh,
        in_specs=placed,
        out_specs=(P(),) * 4,
        check_vma=False,
    )
```

time: 57.9 us -> 45 us (0.78)
  Pallas kernels: 14.8 us -> 9.95 us
  local copies, waits for them, and re-layouts: 4.25 us -> 0.05 us
  blocking collectives: 29.8 us -> 27.4 us
  waiting for transfers between devices: 3.77 us -> 2.1 us
    pallas_call x4 -> x10, Pallas kernels: 14.8 us -> 9.95 us  [call(): pl.pallas_call(kernel, out_shape=out, in_specs=specs or [VMEM] * len(inpu...]
    dynamic_slice x4 -> x0, local copies, waits for them, and re-layouts: 2.28 us -> none  [the longest x2 1.56 us: on_device(): lax.dynamic_index_in_dim(g2[0], section, 0, False)]
    unnamed x12 -> x0, local copies, waits for them, and re-layouts: 1.94 us -> none
    all_to_all x1, blocking collectives: 19.1 us -> 17.5 us  [on_device(): parts = lax.all_to_all(packed, axes, 0, 0, tiled=True)]
    ppermute x2, waiting for transfers between devices: 2.34 us -> 1.09 us  [on_device(): lax.ppermute(v, 'space', pairs_of((size, GY), grid_z, k))]
    all_to_all x1, blocking collectives: 10.7 us -> 9.91 us  [on_device(): total = lax.all_to_all(mine, axes, 0, 0, tiled=True)]
  transfers between devices with their start and end apart: 5 -> 6, of which waited for: 2 -> 2; matrix products, arithmetic and copies ran while one was open for 0% -> 0% of each run, Pallas kernels for 0% -> 8%
where the time goes in v3:
time: 45 us; the launch traced here: 44.8 us
  blocking collectives  27.4 us (61%)
  Pallas kernels  9.95 us (22%)
  starting transfers between devices  4.58 us (10%)
  waiting for transfers between devices  2.1 us (5%)
  between operations  0.71 us (2%)
    all_to_all x1, blocking collectives, on_device(): parts = lax.all_to_all(packed, axes, 0, 0, tiled=True)  17.5 us
    pallas_call x10, Pallas kernels, call(): pl.pallas_call(kernel, out_shape=out, in_specs=specs or [VMEM] * len(inpu...  9.95 us
    all_to_all x1, blocking collectives, on_device(): total = lax.all_to_all(mine, axes, 0, 0, tiled=True)  9.91 us
    ppermute x2, starting transfers between devices, on_device(): lax.ppermute(v, 'space', pairs_of((size, GY), grid_z, k))  3.71 us
    ppermute x2, waiting for transfers between devices, on_device(): lax.ppermute(v, 'space', pairs_of((size, GY), grid_z, k))  1.09 us
    ppermute x3, waiting for transfers between devices, on_device(): lax.ppermute(v, 'space', pairs_of((size, grid_z), 1, k // 3))  1 us
  transfers between devices with their start and end apart: 6, of which 2 were waited for; matrix products, arithmetic and copies ran while one was open for 0% of the time, Pallas kernels for 8%

profile of v3, /device:TPU:0, one launch (start us, length us, event | category | flops | bytes accessed | tf_op | source)
XLA Modules:
  0.0 44.8 jit_solution(16214073984892804504)
XLA Ops:
  0.6 1.2 %fetch.1 = (bf16[4,8,8,256]{3,2,1,0:T(8,128)(2,1)S(1)}, bf16[32,4,4,128]{3,2,1,0:T(4,128)(2,1)S(1)}, bf16[64,2,2,64]{3,2,1,0:T(2,128)(2,1)S(1)}, bf16[27,4,32]{2...) custom-call(bf16[1,2,4,8,8,256]{5,4,3,2,1,0:T(8,128)(2,1)} %refs_0_.1, ...), custom_call_target="tpu_custom_call" | custom-call | tf_op jit(solution)/shard_map/fetch/pallas_call | solution.py:362
  1.9 0.1 y_pack.1
  2.0 3.1 %collective-permute-start = (bf16[384,128]{1,0:T(8,128)(2,1)S(1)}, bf16[384,128]{1,0:T(8,128)(2,1)S(1)}, u32[]{:S(2)}, u32[]{:S(2)}) collective-permute-start(bf16[384,128]{1,0:T(8,128)(2,1)S(1)} %get-tuple-element.50), channel_id=1, source_target_pairs={{0,2},{1,3},{2,0},{3,1},{4,6},{5,7},{6,4},{7,5},{8,10},{9,11},{10,... | collective-permute-start | bytes 294920 | tf_op jit(solution)/shard_map/ppermute | solution.py:405
  5.1 0.7 %collective-permute-start.1 = (bf16[384,128]{1,0:T(8,128)(2,1)S(1)}, bf16[384,128]{1,0:T(8,128)(2,1)S(1)}, u32[]{:S(2)}, u32[]{:S(2)}) collective-permute-start(bf16[384,128]{1,0:T(8,128)(2,1)S(1)} %get-tuple-element.51), channel_id=1, source_target_pairs={{2,4},{3,5},{4,2},{5,3},{6,8},{7,9},{8,6},{9,7},{10,12},{11,13},{1... | collective-permute-start | bytes 294920 | tf_op jit(solution)/shard_map/ppermute | solution.py:405
  5.7 1.0 %prep.1 = (bf16[768,1024]{1,0:T(8,128)(2,1)S(1)}, bf16[432,2048]{1,0:T(8,128)(2,1)S(1)}, bf16[3,384,768]{2,1,0:T(8,128)(2,1)S(1)}, bf16[3,128,1152]{2,1,0:T(8,12...) custom-call(bf16[4,4,32,128]{3,2,1,0:T(8,128)(2,1)S(1)} %bitcast.23,, ...), custom_call_target="tpu_custom_call" | custom-call | tf_op jit(solution)/shard_map/prep/pallas_call | solution.py:362
  6.8 1.1 %collective-permute-done.ra_ref = bf16[384,128]{1,0:T(8,128)(2,1)S(1)} collective-permute-done((bf16[384,128]{1,0:T(8,128)(2,1)S(1)}, bf16[384,128]{1,0:T(8,128)(2,1)S(1)}, u32[]{:S(2)}, u32[]{:S(2)}) %collective-permute-start) | collective-permute-done | bytes 98336 | tf_op jit(solution)/shard_map/ppermute | solution.py:405
  7.9 0.0 collective-permute-done.1.rb_ref
  7.9 0.2 z_pack.1
  8.1 0.1 collective-permute-start.2
  8.1 0.5 %collective-permute-start.4 = (bf16[16,2560]{1,0:T(8,128)(2,1)S(1)}, bf16[16,2560]{1,0:T(8,128)(2,1)S(1)}, u32[]{:S(2)}, u32[]{:S(2)}) collective-permute-start(bf16[16,2560]{1,0:T(8,128)(2,1)S(1)} %get-tuple-element.60), channel_id=1, source_target_pairs={{0,1},{1,0},{2,3},{3,2},{4,5},{5,4},{6,7},{7,6},{8,9},{9,8},{10,11... | collective-permute-start | bytes 245768 | tf_op jit(solution)/shard_map/ppermute | solution.py:432
  8.6 0.1 collective-permute-start.3
  8.7 0.2 rims_in.1
  8.9 1.0 %collective-permute-done.3.refs_5_ = bf16[4,64,64]{2,1,0:T(8,128)(2,1)S(1)} collective-permute-done((bf16[4,64,64]{2,1,0:T(8,128)(2,1)S(1)}, bf16[4,64,64]{2,1,0:T(8,128)(2,1)S(1)}, u32[]{:S(2)}, u32[]{:S(2)}) %collective-permute-start.3) | collective-permute-done | bytes 32800 | tf_op jit(solution)/shard_map/ppermute | solution.py:432
  9.9 0.0 collective-permute-done.4.refs_6_.refs_7_
  9.9 0.0 collective-permute-done.2.refs_4_
  9.9 3.5 %second_grads.1 = (bf16[768,1024]{1,0:T(8,128)(2,1)S(1)}, bf16[1152,768]{1,0:T(8,128)(2,1)S(1)}, f32[216,128]{1,0:T(8,128)S(1)}, f32[216,128]{1,0:T(8,128)S(1)}, f32[8,64]{1,0:T(8,128)S(1)}) custom-call(bf16[768,1024]{1,0:T(8,128)(2,1)S(1)} %get-tuple-element.54.refs_0_, ...), custom_call_target="tpu_custom_call", output_to_operand_aliasing={{0}: (0, {})} | custom-call | tf_op jit(solution)/shard_map/second_grads/pallas_call | solution.py:362
  13.4 0.2 collective-permute-start.5
  13.6 2.6 %first_grads.1 = (bf16[432,2048]{1,0:T(8,128)(2,1)S(1)}, f32[40,128]{1,0:T(8,128)S(1)}, f32[8,32]{1,0:T(8,128)S(1)}) custom-call(bf16[432,2048]{1,0:T(8,128)(2,1)S(1)} %get-tuple-element.64.refs_0_, bf16[1152,768]{1,0:T(8,128)(2,1)S(1)} %get-tuple-element.65.refs_1_, ...), custom_call_target="tpu_custom_call", output_to_operand_aliasing={{0}: (0, {})} | custom-call | tf_op jit(solution)/shard_map/first_grads/pallas_call | solution.py:362
  16.2 0.0 collective-permute-done.5.got_ref
  16.2 0.1 pack_grads.1
  16.3 17.5 %all_to_all.10.parts_ref = f32[32,8,128]{2,1,0:T(8,128)S(1)} all-to-all(f32[32,8,128]{2,1,0:T(8,128)S(1)} %pack_grads.1), channel_id=1, replica_groups=mesh['section'=2,'space'=16] {'section','space'}, dimensions={0} | all-to-all | bytes 262144 | tf_op jit(solution)/shard_map/all_to_all | solution.py:477
  33.9 9.9 %all_to_all.11.sum_ref = bf16[32,2,8,128]{3,2,1,0:T(8,128)(2,1)S(1)} all-to-all(bf16[32,2,8,128]{3,2,1,0:T(8,128)(2,1)S(1)} %sum_parts.1), channel_id=1, replica_groups=mesh['section'=2,'space'=16] {'section','space'}, dimensions={0} | all-to-all | bytes 262144 | tf_op jit(solution)/shard_map/all_to_all | solution.py:484
  43.8 1.0 %unpack.1 = (f32[27,4,32]{2,1,0:T(4,128)}, f32[1,32]{1,0:T(1,128)}, f32[864,64]{1,0:T(8,128)}, f32[1,64]{1,0:T(1,128)}) custom-call(bf16[32,2,8,128]{3,2,1,0:T(8,128)(2,1)S(1)} %all_to_all.11.sum_ref), custom_call_target="tpu_custom_call" | custom-call | tf_op jit(solution)/shard_map/unpack/pallas_call | solution.py:362
  (3 shorter events, 0.1 us)
Async XLA Ops:
  2.0 5.9 %collective-permute-start = (bf16[384,128]{1,0:T(8,128)(2,1)S(1)}, bf16[384,128]{1,0:T(8,128)(2,1)S(1)}, u32[]{:S(2)}, u32[]{:S(2)}) collective-permute-start(bf16[384,128]{1,0:T(8,128)(2,1)S(1)} %get-tuple-element.50), channel_id=1, source_target_pairs={{0,2},{1,3},{2,0},{3,1},{4,6},{5,7},{6,4},{7,5},{8,10},{9,11},{10,... | collective-permute-start | bytes 294920 | tf_op jit(solution)/shard_map/ppermute | solution.py:405
  5.1 2.8 %collective-permute-start.1 = (bf16[384,128]{1,0:T(8,128)(2,1)S(1)}, bf16[384,128]{1,0:T(8,128)(2,1)S(1)}, u32[]{:S(2)}, u32[]{:S(2)}) collective-permute-start(bf16[384,128]{1,0:T(8,128)(2,1)S(1)} %get-tuple-element.51), channel_id=1, source_target_pairs={{2,4},{3,5},{4,2},{5,3},{6,8},{7,9},{8,6},{9,7},{10,12},{11,13},{1... | collective-permute-start | bytes 294920 | tf_op jit(solution)/shard_map/ppermute | solution.py:405
  8.1 1.8 %collective-permute-start.2 = (bf16[8,2,32,128]{3,2,1,0:T(8,128)(2,1)S(1)}, bf16[8,2,32,128]{3,2,1,0:T(8,128)(2,1)S(1)}, u32[]{:S(2)}, u32[]{:S(2)}) collective-permute-start(bf16[8,2,32,128]{3,2,1,0:T(8,128)(2,1)S(1)} %get-tuple-element.58), channel_id=1, source_target_pairs={{0,1},{1,0},{2,3},{3,2},{4,5},{5,4},{6,7},{7,6},{8,9},{9,8},{10,11... | collective-permute-start | bytes 393224 | tf_op jit(solution)/shard_map/ppermute | solution.py:432
  8.1 1.8 %collective-permute-start.4 = (bf16[16,2560]{1,0:T(8,128)(2,1)S(1)}, bf16[16,2560]{1,0:T(8,128)(2,1)S(1)}, u32[]{:S(2)}, u32[]{:S(2)}) collective-permute-start(bf16[16,2560]{1,0:T(8,128)(2,1)S(1)} %get-tuple-element.60), channel_id=1, source_target_pairs={{0,1},{1,0},{2,3},{3,2},{4,5},{5,4},{6,7},{7,6},{8,9},{9,8},{10,11... | collective-permute-start | bytes 245768 | tf_op jit(solution)/shard_map/ppermute | solution.py:432
  8.6 1.3 %collective-permute-start.3 = (bf16[4,64,64]{2,1,0:T(8,128)(2,1)S(1)}, bf16[4,64,64]{2,1,0:T(8,128)(2,1)S(1)}, u32[]{:S(2)}, u32[]{:S(2)}) collective-permute-start(bf16[4,64,64]{2,1,0:T(8,128)(2,1)S(1)} %get-tuple-element.59), channel_id=1, source_target_pairs={{0,1},{1,0},{2,3},{3,2},{4,5},{5,4},{6,7},{7,6},{8,9},{9,8},{10,11... | collective-permute-start | bytes 98312 | tf_op jit(solution)/shard_map/ppermute | solution.py:432
  13.4 2.8 %collective-permute-start.5 = (f32[216,128]{1,0:T(8,128)S(1)}, f32[216,128]{1,0:T(8,128)S(1)}, u32[]{:S(2)}, u32[]{:S(2)}) collective-permute-start(f32[216,128]{1,0:T(8,128)S(1)} %get-tuple-element.62), channel_id=1, source_target_pairs={{0,1},{1,0},{2,3},{3,2},{4,5},{5,4},{6,7},{7,6},{8,9},{9,8},{10,11... | collective-permute-start | bytes 331784 | tf_op jit(solution)/shard_map/ppermute | solution.py:456

commit v4 on v3

--- a/solution.py
+++ b/solution.py
@@ -108,17 +108,18 @@
         x0r_ref[side, :, 128:] = rim[352:384]
     g2y_ref[1:3] = g2_ref[...]
     zpar = z_parity(grid_z)
-    for k in range(len(sends) // 3):
-        sx1_ref, sg2_ref, sx0_ref = sends[3 * k : 3 * k + 3]
+    for k, send_ref in enumerate(sends):
         up = 1 - zpar if k == 0 else zpar
         for y in range(8):
             for p in range(2):
                 if 2 <= y < 6:
-                    sx1_ref[y, p] = x1_ref[y - 2, up * 2 + p]
+                    plane = x1_ref[y - 2, up * 2 + p]
                 else:
-                    sx1_ref[y, p] = x1r_ref[y if y < 2 else y - 4, up * 2 + p]
-        for y in range(4):
-            sg2_ref[y] = g2y_ref[y, up]
+                    plane = x1r_ref[y if y < 2 else y - 4, up * 2 + p]
+                send_ref[(y * 2 + p) * 32 : (y * 2 + p + 1) * 32, :] = plane
+        for y in range(0, 4, 2):
+            pair = jnp.concatenate([g2y_ref[y, up], g2y_ref[y + 1, up]], axis=1)
+            send_ref[512 + y * 32 : 576 + y * 32, :] = pair
         row = lax.broadcasted_iota(jnp.int32, (16, 32), 0)
         col = lax.broadcasted_iota(jnp.int32, (16, 32), 1)
         take = jnp.where((col == row * 8 + up * 7) & (row < 4), 1.0, 0.0).astype(BF)
@@ -127,7 +128,9 @@
                 block = jnp.concatenate([x0_ref[i, y - 1] for i in range(4)], axis=0)
             else:
                 block = x0r_ref[0 if y == 0 else 1]
-            sx0_ref[:, y * 256 : y * 256 + 256] = dot(take, block).astype(BF)
+            plane = dot(take, block).astype(BF)
+            send_ref[640 + y * 32 : 656 + y * 32, :] = plane[:, :128]
+            send_ref[656 + y * 32 : 672 + y * 32, :] = plane[:, 128:]
 
 
 def put_second(xs, y, z, block):
@@ -146,7 +149,7 @@
 
 def prep(
     x1_ref, x0_ref, w1_ref, b1_ref, w2_ref, b2_ref,
-    xs, x0s, wb2, wd, wb0, b1_out, b2_out, fold, zcol, w1f,
+    xs, x0s, wb2, wd, wb0, b1_out, b2_out, w1f,
 ):
     for y in range(4):
         for z in range(4):
@@ -158,7 +161,7 @@
     wd[...] = jnp.zeros_like(wd)
     for a in range(3):
         w2t = jnp.transpose(w2_ref[a * 288 : a * 288 + 288, :].astype(F32)).astype(BF)
-        for z in range(6):
+        for z in range(3):
             wb2[a, z * 64 : z * 64 + 64, z * 96 : z * 96 + 288] = w2t
         for b in range(3):
             for c in range(3):
@@ -169,10 +172,6 @@
                     wd[a, z * 32 : z * 32 + 32, at : at + 64] = value
     b2_out[...] = jnp.transpose(jnp.broadcast_to(b2_ref[...], (128, 64)))
     b1_out[...] = jnp.transpose(jnp.broadcast_to(b1_ref[...], (128, 32)))
-    block, chan, plane = place_of(lax.broadcasted_iota(jnp.int32, fold.shape, 1))
-    row = lax.broadcasted_iota(jnp.int32, fold.shape, 0)
-    fold[...] = jnp.where((row == block * 4 + chan) & (plane >= 0), 1.0, 0.0)
-    zcol[...] = place_of(lax.broadcasted_iota(jnp.int32, zcol.shape, 0))[2].astype(F32)
     w1f[108:112, :] = jnp.zeros((4, 32), F32)
     for k in range(27):
         w1f[k * 4 : k * 4 + 4, :] = w1_ref[k].astype(F32)
@@ -198,12 +197,12 @@
         put_first(x0s, y, 0, x0r_ref[k])
 
 
-def rims_of(grid_z, kinds, got):
+def rims_of(grid_z, got):
     even = z_parity(grid_z) == 0
 
-    def rims(ref, index):
-        one = got[ref][index]
-        two = got[len(got) // 2 + ref][index] if kinds == 2 else jnp.zeros_like(one)
+    def rims(start, size):
+        one = got[0][start : start + size]
+        two = got[1][start : start + size] if len(got) == 2 else jnp.zeros_like(one)
         return jnp.where(even, two, one), jnp.where(even, one, two)
 
     return rims
@@ -211,46 +210,54 @@
 
 def second_grads(grid_z, kinds, *refs):
     xs_in, wb2, b2_ref, g2y_ref = refs[:4]
-    rims = rims_of(grid_z, kinds, refs[4 : 4 + 3 * kinds])
-    xs, ds, keep_ref, send_ref, bias_ref, dz1 = refs[4 + 3 * kinds :]
+    rims = rims_of(grid_z, refs[4 : 4 + kinds])
+    xs, ds, keep_ref, send_ref, bias_ref, dz1 = refs[4 + kinds :]
 
     for y in range(8):
         for p in range(2):
-            low, high = rims(0, (y, p))
+            low, high = rims((y * 2 + p) * 32, 32)
             put_second(xs, y, p, low)
             put_second(xs, y, 6 + p, high)
 
     twice = doubler(64)
     coarse = []
-    rim = [rims(1, (y,)) for y in range(4)]
+    rim = [rims(512 + y * 64, 64) for y in range(2)]
     for z in range(4):
-        plane = [
-            rim[y][0] if z == 0 else rim[y][1] if z == 3 else g2y_ref[y, z - 1] for y in range(4)
-        ]
+        plane = []
+        for y in range(4):
+            if z in (0, 3):
+                plane.append(rim[y // 2][z // 3][:, (y % 2) * 64 : (y % 2) * 64 + 64])
+            else:
+                plane.append(g2y_ref[y, z - 1])
         coarse.append(dot(jnp.concatenate(plane, axis=0), twice))
     b2c = b2_ref[...]
-    for half in range(3):
-        pre = dot(wb2[0], xs[:, half * 256 : half * 256 + 256])
-        pre += dot(wb2[1], xs[:, half * 256 + 128 : half * 256 + 384])
-        pre += dot(wb2[2], xs[:, half * 256 + 256 : half * 256 + 512])
-        for y in (2 * half, 2 * half + 1):
-            at = (y + 1) // 2 * 64
-            for z in range(6):
-                grad = coarse[(z + 1) // 2][at : at + 64]
-                here = pre[z * 64 : z * 64 + 64, (y % 2) * 128 : (y % 2) * 128 + 128] + b2c
-                delta = (grad * jnp.where(here > 0, 0.125, LOW)).astype(BF)
-                dz1[z * 64 : z * 64 + 64, y * 128 : y * 128 + 128] = delta
-                for c, value in enumerate(shifts(delta)):
-                    row = z * 192 + c * 64
-                    ds[row : row + 64, y * 128 : y * 128 + 128] = value
+    for part in range(3):
+        for group in range(2):
+            rows = slice(group * 288, group * 288 + 480)
+            pre = dot(wb2[0], xs[rows, part * 256 : part * 256 + 256])
+            pre += dot(wb2[1], xs[rows, part * 256 + 128 : part * 256 + 384])
+            pre += dot(wb2[2], xs[rows, part * 256 + 256 : part * 256 + 512])
+            for y in (2 * part, 2 * part + 1):
+                at = (y + 1) // 2 * 64
+                for k in range(3):
+                    z = group * 3 + k
+                    grad = coarse[(z + 1) // 2][at : at + 64]
+                    here = pre[k * 64 : k * 64 + 64, (y % 2) * 128 : (y % 2) * 128 + 128] + b2c
+                    delta = (grad * jnp.where(here > 0, 0.125, LOW)).astype(BF)
+                    dz1[z * 64 : z * 64 + 64, y * 128 : y * 128 + 128] = delta
+                    for c, value in enumerate(shifts(delta)):
+                        row = z * 192 + c * 64
+                        ds[row : row + 64, y * 128 : y * 128 + 128] = value
 
     own = dz1[64:320, 128:640]
     line = dot_nt(jnp.ones((8, 512), BF), own)
     bias_ref[...] = sum(line[:, z * 64 : z * 64 + 64] for z in range(4))
     parts = []
     for a in range(3):
-        full = dot_nt(xs[96:672, (a + 1) * 128 : (a + 5) * 128], own)
-        parts.append(sum(full[z * 96 : z * 96 + 288, z * 64 : z * 64 + 64] for z in range(4)))
+        lanes = slice((a + 1) * 128, (a + 5) * 128)
+        full = dot_nt(xs[96:480, lanes], own[:128])
+        full += dot_nt(xs[288:672, lanes], own[128:])
+        parts.append(full[:288, :64] + full[96:, 64:])
     even = z_parity(grid_z) == 0
     low = (parts[0][:216], jnp.concatenate([parts[0][216:], parts[1][:144]], axis=0))
     high = (jnp.concatenate([parts[1][144:], parts[2][:72]], axis=0), parts[2][72:])
@@ -260,9 +267,9 @@
 
 
 def first_grads(grid_z, kinds, *refs):
-    x0s_in, ds, wd, wb0, b1_ref, fold_ref, zcol_ref = refs[:7]
-    rims = rims_of(grid_z, kinds, refs[7 : 7 + kinds])
-    x0s, out_ref, line_ref, dz0, up = refs[7 + kinds :]
+    x0s_in, ds, wd, wb0, b1_ref = refs[:5]
+    rims = rims_of(grid_z, refs[5 : 5 + kinds])
+    x0s, out_ref, line_ref, dz0, up = refs[5 + kinds :]
 
     back = dot(wd[0], ds[:, :512])
     back += dot(wd[1], ds[:, 128:640])
@@ -271,11 +278,11 @@
     stack = [back[:, y * 128 : y * 128 + 128] for y in range(4)]
     up[...] = dot(jnp.concatenate(stack, axis=0), doubler(128))
 
-    low, high = rims(0, Ellipsis)
     ones = jnp.where(lax.broadcasted_iota(jnp.int32, (8, 256), 0) == 0, 1.0, 0.0)
     for y in range(10):
-        lanes = slice(y * 256, y * 256 + 256)
-        pair = jnp.concatenate([low[:4, lanes].astype(F32), high[:4, lanes].astype(F32)], axis=0)
+        halves = [rims(640 + y * 32 + h * 16, 16) for h in range(2)]
+        low, high = (jnp.concatenate([h[k] for h in halves], axis=1) for k in range(2))
+        pair = jnp.concatenate([low[:4].astype(F32), high[:4].astype(F32)], axis=0)
         put_first(x0s, y, 32, jnp.concatenate([pair, ones], axis=0).astype(BF))
 
     b1w = jnp.concatenate([b1_ref[...], b1_ref[...]], axis=1)
@@ -289,24 +296,24 @@
             dz0[z * 32 : z * 32 + 32, lanes] = delta.astype(BF)
 
     full = dot_nt(x0s[...], dz0[...])
-    zcol = zcol_ref[...]
-    lane = lax.broadcasted_iota(jnp.int32, zcol.shape, 1)
-    zlane = lax.shift_right_logical(lane, 5).astype(F32)
-    every = []
-    for b in range(3):
-        part = jnp.where(zcol == zlane + b, full[:, :128], 0.0)
-        part += jnp.where(zcol == zlane + (b + 4), full[:, 128:], 0.0)
-        part += pltpu.roll(part, 64, 1)
-        every.append(part + pltpu.roll(part, 32, 1))
-    part = jnp.where(lane < 32, every[0], jnp.where(lane < 64, every[1], every[2]))
-    part = lax.dot_general(
-        fold_ref[...],
-        part,
-        (((1,), (0,)), ((), ())),
-        precision=lax.Precision.HIGHEST,
-        preferred_element_type=F32,
-    )
-    out_ref[...] = part
+    row = lax.broadcasted_iota(jnp.int32, (8, 256), 0)
+    lane = lax.shift_right_logical(lax.broadcasted_iota(jnp.int32, (8, 256), 1), 5)
+    band = (lane >= row - 1) & (lane <= row + 1)
+    ends = jnp.where(row < 4, 0, 7) == lane
+    odd = (row[:, :128] & 1) == 1
+    upper = (row[:, :128] & 2) == 2
+    out_ref[36:, :] = jnp.zeros((4, 128), F32)
+    for block in range(9):
+        edge = jnp.where(ends, full[block * SPAN + 32 : block * SPAN + 40], 0.0)
+        edge = edge[:, :128] + edge[:, 128:]
+        edge = pltpu.roll(edge[:4], 32, 1) + edge[4:]
+        for i in range(4):
+            part = jnp.where(band, full[block * SPAN + i * 8 : block * SPAN + i * 8 + 8], 0.0)
+            part = part[:, :128] + part[:, 128:]
+            part = jnp.where(odd, pltpu.roll(part, 96, 1), part)
+            part = jnp.where(upper, pltpu.roll(part, 64, 1), part)
+            part = jnp.sum(part, axis=0, keepdims=True) + edge[i : i + 1]
+            out_ref[block * 4 + i : block * 4 + i + 1, :] = part
     line = full[4 * SPAN + 40 : 4 * SPAN + 48]
     line_ref[...] = sum(line[:, z * 32 : z * 32 + 32] for z in range(8))
 
@@ -315,9 +322,9 @@
     flat[...] = jnp.zeros_like(flat)
     flat[:216, :] = keep_ref[...] + got_ref[...]
     at = (deep - 1) * count
-    flat[at : at + 27, :96] = part_ref[:27, :96]
-    for b in range(3):
-        flat[at + b * 9 : at + b * 9 + 9, 96:] = part_ref[27:36, b * 32 : b * 32 + 32]
+    for b, lane in enumerate((32, 0, 96)):
+        flat[at : at + 27, b * 32 : b * 32 + 32] = part_ref[:27, lane : lane + 32]
+        flat[at + b * 9 : at + b * 9 + 9, 96:] = part_ref[27:36, lane : lane + 32]
     flat[at + 27 : at + 28, :64] = bias_two_ref[:1, :]
     flat[at + 27 : at + 28, 64:96] = bias_one_ref[:1, :]
     for k in range(deep):
@@ -403,25 +410,23 @@
         functools.partial(y_pack, grid_z), (shaped(384, 128),) * 2, (x1, g2, x0), name="y_pack"
     )
     got = [lax.ppermute(v, "space", pairs_of((size, GY), grid_z, k)) for k, v in enumerate(send)]
-    xs, x0s, wb2, wd, wb0, b1, b2, fold, zcol = call(
+    xs, x0s, wb2, wd, wb0, b1, b2 = call(
         prep,
         (
             shaped(768, 1024),
             shaped(9 * SPAN, 2048),
-            shaped(3, 384, 768),
+            shaped(3, 192, 480),
             shaped(3, 128, 1152),
             shaped(256, 9 * SPAN),
             shaped(32, 128, dtype=F32),
             shaped(64, 128, dtype=F32),
-            shaped(40, 9 * SPAN, dtype=F32),
-            shaped(9 * SPAN, 128, dtype=F32),
         ),
         (x1, x0, w1, b1, w2, b2),
         scratch=(pltpu.VMEM((112, 32), F32),),
         name="prep",
     )
     kinds = 1 if grid_z == 2 else 2
-    sends = (shaped(8, 2, 32, 128), shaped(4, 64, 64), shaped(16, 2560)) * kinds
+    sends = (shaped(960, 128),) * kinds
     wide = call(
         functools.partial(z_pack, grid_z),
         (shaped(4, 4, 32, 128), shaped(4, 2, 64, 64), shaped(2, 32, 256)) + sends,
@@ -429,7 +434,7 @@
         name="z_pack",
     )
     rims = [
-        lax.ppermute(v, "space", pairs_of((size, grid_z), 1, k // 3))
+        lax.ppermute(v, "space", pairs_of((size, grid_z), 1, k))
         for k, v in enumerate(wide[3:])
     ]
     xs, x0s = call(
@@ -457,7 +462,7 @@
     x0s, part_one, line_one = call(
         functools.partial(first_grads, grid_z, kinds),
         (shaped(9 * SPAN, 2048), shaped(40, 128, dtype=F32), shaped(8, 32, dtype=F32)),
-        (x0s, ds, wd, wb0, b1, fold, zcol, *rims[2::3]),
+        (x0s, ds, wd, wb0, b1, *rims),
         scratch=(pltpu.VMEM((256, 2048), BF), pltpu.VMEM((512, 256), F32)),
         alias={0: 0},
         name="first_grads",

time: 45 us -> 43 us (0.956)
  Pallas kernels: 9.95 us -> 8.03 us
  starting transfers between devices: 4.58 us -> 3.98 us
  waiting for transfers between devices: 2.1 us -> 2.6 us
    pallas_call x10, Pallas kernels: 9.95 us -> 8.03 us  [call(): pl.pallas_call(kernel, out_shape=out, in_specs=specs or [VMEM] * len(inpu...]
    ppermute x3 -> x1, starting transfers between devices: 0.65 us -> 0.07 us  [on_device(): lax.ppermute(v, 'space', pairs_of((size, grid_z), 1, k))]
    ppermute x3 -> x1, waiting for transfers between devices: 1 us -> 1.31 us  [on_device(): lax.ppermute(v, 'space', pairs_of((size, grid_z), 1, k))]
  transfers between devices with their start and end apart: 6 -> 4, of which waited for: 2 -> 2; matrix products, arithmetic and copies ran while one was open for 0% -> 0% of each run, Pallas kernels for 8% -> 7%
where the time goes in v4:
time: 43 us; the launch traced here: 42.8 us
  blocking collectives  27.4 us (64%)
  Pallas kernels  8.03 us (19%)
  starting transfers between devices  3.98 us (9%)
  waiting for transfers between devices  2.6 us (6%)
  between operations  0.71 us (2%)
    all_to_all x1, blocking collectives, on_device(): parts = lax.all_to_all(packed, axes, 0, 0, tiled=True)  17.5 us
    all_to_all x1, blocking collectives, on_device(): total = lax.all_to_all(mine, axes, 0, 0, tiled=True)  9.91 us
    pallas_call x10, Pallas kernels, call(): pl.pallas_call(kernel, out_shape=out, in_specs=specs or [VMEM] * len(inpu...  8.03 us
    ppermute x2, starting transfers between devices, on_device(): lax.ppermute(v, 'space', pairs_of((size, GY), grid_z, k))  3.71 us
    ppermute x1, waiting for transfers between devices, on_device(): lax.ppermute(v, 'space', pairs_of((size, grid_z), 1, k))  1.31 us
    ppermute x2, waiting for transfers between devices, on_device(): lax.ppermute(v, 'space', pairs_of((size, GY), grid_z, k))  1.28 us
  transfers between devices with their start and end apart: 4, of which 2 were waited for; matrix products, arithmetic and copies ran while one was open for 0% of the time, Pallas kernels for 7%

profile of v4, /device:TPU:0, one launch (start us, length us, event | category | flops | bytes accessed | tf_op | source)
XLA Modules:
  0.0 42.8 jit_solution(12444041746203797899)
XLA Ops:
  0.6 1.2 %fetch.1 = (bf16[4,8,8,256]{3,2,1,0:T(8,128)(2,1)S(1)}, bf16[32,4,4,128]{3,2,1,0:T(4,128)(2,1)S(1)}, bf16[64,2,2,64]{3,2,1,0:T(2,128)(2,1)S(1)}, bf16[27,4,32]{2...) custom-call(bf16[1,2,4,8,8,256]{5,4,3,2,1,0:T(8,128)(2,1)} %refs_0_.1, ...), custom_call_target="tpu_custom_call" | custom-call | tf_op jit(solution)/shard_map/fetch/pallas_call | solution.py:369
  1.9 0.1 y_pack.1
  2.0 3.1 %collective-permute-start = (bf16[384,128]{1,0:T(8,128)(2,1)S(1)}, bf16[384,128]{1,0:T(8,128)(2,1)S(1)}, u32[]{:S(2)}, u32[]{:S(2)}) collective-permute-start(bf16[384,128]{1,0:T(8,128)(2,1)S(1)} %get-tuple-element.46), channel_id=1, source_target_pairs={{0,2},{1,3},{2,0},{3,1},{4,6},{5,7},{6,4},{7,5},{8,10},{9,11},{10,... | collective-permute-start | bytes 294920 | tf_op jit(solution)/shard_map/ppermute | solution.py:412
  5.1 0.7 %collective-permute-start.1 = (bf16[384,128]{1,0:T(8,128)(2,1)S(1)}, bf16[384,128]{1,0:T(8,128)(2,1)S(1)}, u32[]{:S(2)}, u32[]{:S(2)}) collective-permute-start(bf16[384,128]{1,0:T(8,128)(2,1)S(1)} %get-tuple-element.47), channel_id=1, source_target_pairs={{2,4},{3,5},{4,2},{5,3},{6,8},{7,9},{8,6},{9,7},{10,12},{11,13},{1... | collective-permute-start | bytes 294920 | tf_op jit(solution)/shard_map/ppermute | solution.py:412
  5.7 0.9 %prep.1 = (bf16[768,1024]{1,0:T(8,128)(2,1)S(1)}, bf16[432,2048]{1,0:T(8,128)(2,1)S(1)}, bf16[3,192,480]{2,1,0:T(8,128)(2,1)S(1)}, bf16[3,128,1152]{2,1,0:T(8,12...) custom-call(bf16[4,4,32,128]{3,2,1,0:T(8,128)(2,1)S(1)} %bitcast.23, ...), custom_call_target="tpu_custom_call" | custom-call | tf_op jit(solution)/shard_map/prep/pallas_call | solution.py:369
  6.6 1.3 %collective-permute-done.ra_ref = bf16[384,128]{1,0:T(8,128)(2,1)S(1)} collective-permute-done((bf16[384,128]{1,0:T(8,128)(2,1)S(1)}, bf16[384,128]{1,0:T(8,128)(2,1)S(1)}, u32[]{:S(2)}, u32[]{:S(2)}) %collective-permute-start) | collective-permute-done | bytes 98336 | tf_op jit(solution)/shard_map/ppermute | solution.py:412
  7.9 0.0 collective-permute-done.1.rb_ref
  7.9 0.2 z_pack.1
  8.1 0.1 collective-permute-start.2
  8.1 0.2 rims_in.1
  8.3 1.3 %collective-permute-done.2.refs_4_.refs_5_ = bf16[960,128]{1,0:T(8,128)(2,1)S(1)} collective-permute-done((bf16[960,128]{1,0:T(8,128)(2,1)S(1)}, bf16[960,128]{1,0:T(8,128)(2,1)S(1)}, u32[]{:S(2)}, u32[]{:S(2)}) %collective-permute-start.2) | collective-permute-done | bytes 245792 | tf_op jit(solution)/shard_map/ppermute | solution.py:437
  9.6 2.3 %second_grads.1 = (bf16[768,1024]{1,0:T(8,128)(2,1)S(1)}, bf16[1152,768]{1,0:T(8,128)(2,1)S(1)}, f32[216,128]{1,0:T(8,128)S(1)}, f32[216,128]{1,0:T(8,128)S(1)}, f32[8,64]{1,0:T(8,128)S(1)}) custom-call(bf16[768,1024]{1,0:T(8,128)(2,1)S(1)} %get-tuple-element.50.refs_0_, ...), custom_call_target="tpu_custom_call", output_to_operand_aliasing={{0}: (0, {})} | custom-call | tf_op jit(solution)/shard_map/second_grads/pallas_call | solution.py:369
  11.9 0.2 collective-permute-start.3
  12.1 2.0 %first_grads.1 = (bf16[432,2048]{1,0:T(8,128)(2,1)S(1)}, f32[40,128]{1,0:T(8,128)S(1)}, f32[8,32]{1,0:T(8,128)S(1)}) custom-call(bf16[432,2048]{1,0:T(8,128)(2,1)S(1)} %get-tuple-element.58.refs_0_, bf16[1152,768]{1,0:T(8,128)(2,1)S(1)} %get-tuple-element.59.refs_1_, ...), custom_call_target="tpu_custom_call", output_to_operand_aliasing={{0}: (0, {})} | custom-call | tf_op jit(solution)/shard_map/first_grads/pallas_call | solution.py:369
  14.2 0.0 collective-permute-done.3.got_ref
  14.2 0.1 pack_grads.1
  14.3 17.5 %all_to_all.10.parts_ref = f32[32,8,128]{2,1,0:T(8,128)S(1)} all-to-all(f32[32,8,128]{2,1,0:T(8,128)S(1)} %pack_grads.1), channel_id=1, replica_groups=mesh['section'=2,'space'=16] {'section','space'}, dimensions={0} | all-to-all | bytes 262144 | tf_op jit(solution)/shard_map/all_to_all | solution.py:482
  31.8 9.9 %all_to_all.11.sum_ref = bf16[32,2,8,128]{3,2,1,0:T(8,128)(2,1)S(1)} all-to-all(bf16[32,2,8,128]{3,2,1,0:T(8,128)(2,1)S(1)} %sum_parts.1), channel_id=1, replica_groups=mesh['section'=2,'space'=16] {'section','space'}, dimensions={0} | all-to-all | bytes 262144 | tf_op jit(solution)/shard_map/all_to_all | solution.py:489
  41.7 1.0 %unpack.1 = (f32[27,4,32]{2,1,0:T(4,128)}, f32[1,32]{1,0:T(1,128)}, f32[864,64]{1,0:T(8,128)}, f32[1,64]{1,0:T(1,128)}) custom-call(bf16[32,2,8,128]{3,2,1,0:T(8,128)(2,1)S(1)} %all_to_all.11.sum_ref), custom_call_target="tpu_custom_call" | custom-call | tf_op jit(solution)/shard_map/unpack/pallas_call | solution.py:369
  (3 shorter events, 0.1 us)
Async XLA Ops:
  2.0 5.9 %collective-permute-start = (bf16[384,128]{1,0:T(8,128)(2,1)S(1)}, bf16[384,128]{1,0:T(8,128)(2,1)S(1)}, u32[]{:S(2)}, u32[]{:S(2)}) collective-permute-start(bf16[384,128]{1,0:T(8,128)(2,1)S(1)} %get-tuple-element.46), channel_id=1, source_target_pairs={{0,2},{1,3},{2,0},{3,1},{4,6},{5,7},{6,4},{7,5},{8,10},{9,11},{10,... | collective-permute-start | bytes 294920 | tf_op jit(solution)/shard_map/ppermute | solution.py:412
  5.1 2.8 %collective-permute-start.1 = (bf16[384,128]{1,0:T(8,128)(2,1)S(1)}, bf16[384,128]{1,0:T(8,128)(2,1)S(1)}, u32[]{:S(2)}, u32[]{:S(2)}) collective-permute-start(bf16[384,128]{1,0:T(8,128)(2,1)S(1)} %get-tuple-element.47), channel_id=1, source_target_pairs={{2,4},{3,5},{4,2},{5,3},{6,8},{7,9},{8,6},{9,7},{10,12},{11,13},{1... | collective-permute-start | bytes 294920 | tf_op jit(solution)/shard_map/ppermute | solution.py:412
  8.1 1.6 %collective-permute-start.2 = (bf16[960,128]{1,0:T(8,128)(2,1)S(1)}, bf16[960,128]{1,0:T(8,128)(2,1)S(1)}, u32[]{:S(2)}, u32[]{:S(2)}) collective-permute-start(bf16[960,128]{1,0:T(8,128)(2,1)S(1)} %get-tuple-element.54), channel_id=1, source_target_pairs={{0,1},{1,0},{2,3},{3,2},{4,5},{5,4},{6,7},{7,6},{8,9},{9,8},{10,11... | collective-permute-start | bytes 737288 | tf_op jit(solution)/shard_map/ppermute | solution.py:437
  11.9 2.2 %collective-permute-start.3 = (f32[216,128]{1,0:T(8,128)S(1)}, f32[216,128]{1,0:T(8,128)S(1)}, u32[]{:S(2)}, u32[]{:S(2)}) collective-permute-start(f32[216,128]{1,0:T(8,128)S(1)} %get-tuple-element.56), channel_id=1, source_target_pairs={{0,1},{1,0},{2,3},{3,2},{4,5},{5,4},{6,7},{7,6},{8,9},{9,8},{10,11... | collective-permute-start | bytes 331784 | tf_op jit(solution)/shard_map/ppermute | solution.py:461

commit v5 on v4

--- a/solution.py
+++ b/solution.py
@@ -92,10 +92,14 @@
         copy.wait()
 
 
-def z_pack(grid_z, ready_ref, x1_ref, g2_ref, x0_ref, ra_ref, rb_ref, x1r_ref, g2y_ref, x0r_ref, *sends):
-    even = y_parity(grid_z) == 0
+def z_pack(grid_z, x1_ref, g2_ref, x0_ref, ra_ref, rb_ref, x1r_ref, g2y_ref, x0r_ref, *sends):
+    par = y_parity(grid_z)
+    even = par == 0
+    line = lax.div(lax.axis_index("space"), grid_z)
+    inner = (line > 0) & (line < GY - 1)
     ra = ra_ref[...]
-    rb = rb_ref[...]
+    rb = rb_ref[pl.ds(pl.multiple_of(par * 384, 384), 384), :]
+    rb = jnp.where(inner, rb, jnp.zeros_like(rb))
     low = jnp.where(even, rb, ra)
     high = jnp.where(even, ra, rb)
     for side, rim in ((0, low), (1, high)):
@@ -148,7 +152,7 @@
 
 
 def prep(
-    x1_ref, x0_ref, w1_ref, b1_ref, w2_ref, b2_ref,
+    x1_ref, x0_ref, x1r_ref, x0r_ref, w1_ref, b1_ref, w2_ref, b2_ref,
     xs, x0s, wb2, wd, wb0, b1_out, b2_out, w1f,
 ):
     for y in range(4):
@@ -157,6 +161,11 @@
     for y in range(8):
         block = jnp.concatenate([x0_ref[i, y] for i in range(4)], axis=0)
         put_first(x0s, y + 1, 0, block)
+    for k, y in enumerate((0, 1, 6, 7)):
+        for z in range(4):
+            put_second(xs, y, z + 2, x1r_ref[k, z])
+    for k, y in enumerate((0, 9)):
+        put_first(x0s, y, 0, x0r_ref[k])
     wb2[...] = jnp.zeros_like(wb2)
     wd[...] = jnp.zeros_like(wd)
     for a in range(3):
@@ -189,14 +198,6 @@
         wb0[z * 32 : z * 32 + 32, :] = value.astype(BF)
 
 
-def rims_in(xs_in, x0s_in, x1r_ref, x0r_ref, xs, x0s):
-    for k, y in enumerate((0, 1, 6, 7)):
-        for z in range(4):
-            put_second(xs, y, z + 2, x1r_ref[k, z])
-    for k, y in enumerate((0, 9)):
-        put_first(x0s, y, 0, x0r_ref[k])
-
-
 def rims_of(grid_z, got):
     even = z_parity(grid_z) == 0
 
@@ -409,7 +410,26 @@
     send = call(
         functools.partial(y_pack, grid_z), (shaped(384, 128),) * 2, (x1, g2, x0), name="y_pack"
     )
-    got = [lax.ppermute(v, "space", pairs_of((size, GY), grid_z, k)) for k, v in enumerate(send)]
+    inner = [
+        [y * grid_z + z, (y + 1) * grid_z + z] for y in range(1, GY - 2, 2) for z in range(grid_z)
+    ]
+    ends = [[y * grid_z + z, y * grid_z + z + 1] for y in (0, GY - 1) for z in range(0, grid_z, 2)]
+    got = [
+        lax.ppermute(send[0], "space", pairs_of((size, GY), grid_z, 0)),
+        lax.all_gather(send[1], "space", axis_index_groups=inner + ends, tiled=True),
+    ]
+    kinds = 1 if grid_z == 2 else 2
+    sends = (shaped(960, 128),) * kinds
+    wide = call(
+        functools.partial(z_pack, grid_z),
+        (shaped(4, 4, 32, 128), shaped(4, 2, 64, 64), shaped(2, 32, 256)) + sends,
+        (x1, g2, x0, *got),
+        name="z_pack",
+    )
+    rims = [
+        lax.ppermute(v, "space", pairs_of((size, grid_z), 1, k))
+        for k, v in enumerate(wide[3:])
+    ]
     xs, x0s, wb2, wd, wb0, b1, b2 = call(
         prep,
         (
@@ -421,28 +441,9 @@
             shaped(32, 128, dtype=F32),
             shaped(64, 128, dtype=F32),
         ),
-        (x1, x0, w1, b1, w2, b2),
+        (x1, x0, wide[0], wide[2], w1, b1, w2, b2),
         scratch=(pltpu.VMEM((112, 32), F32),),
         name="prep",
-    )
-    kinds = 1 if grid_z == 2 else 2
-    sends = (shaped(960, 128),) * kinds
-    wide = call(
-        functools.partial(z_pack, grid_z),
-        (shaped(4, 4, 32, 128), shaped(4, 2, 64, 64), shaped(2, 32, 256)) + sends,
-        (b1, x1, g2, x0, *got),
-        name="z_pack",
-    )
-    rims = [
-        lax.ppermute(v, "space", pairs_of((size, grid_z), 1, k))
-        for k, v in enumerate(wide[3:])
-    ]
-    xs, x0s = call(
-        rims_in,
-        (shaped(768, 1024), shaped(9 * SPAN, 2048)),
-        (xs, x0s, wide[0], wide[2]),
-        alias={0: 0, 1: 1},
-        name="rims_in",
     )
     xs, ds, keep, swap, line_two = call(
         functools.partial(second_grads, grid_z, kinds),

time: 43 us -> 41.7 us (0.970)
  blocking collectives: 27.4 us -> 26.6 us
  starting transfers between devices: 3.98 us -> 3.33 us
    all_to_all x1, blocking collectives: 17.5 us -> 14.8 us  [on_device(): parts = lax.all_to_all(packed, axes, 0, 0, tiled=True)]
    all_gather x0 -> x1, blocking collectives: none -> 1.93 us  [on_device(): lax.all_gather(send[1], 'space', axis_index_groups=inner + ends, tiled=True)]
    ppermute x2 -> x1, waiting for transfers between devices: 1.28 us -> 2.34 us  [on_device(): lax.ppermute(send[0], 'space', pairs_of((size, GY), grid_z, 0))]
    ppermute x1, waiting for transfers between devices: 1.31 us -> 0.52 us  [on_device(): lax.ppermute(v, 'space', pairs_of((size, grid_z), 1, k))]
    ppermute x2 -> x1, starting transfers between devices: 3.71 us -> 3.06 us  [on_device(): lax.ppermute(send[0], 'space', pairs_of((size, GY), grid_z, 0))]
    pallas_call x10 -> x9, Pallas kernels: 8.03 us -> 7.94 us  [call(): pl.pallas_call(kernel, out_shape=out, in_specs=specs or [VMEM] * len(inpu...]
  transfers between devices with their start and end apart: 4 -> 3, of which waited for: 2 -> 2; matrix products, arithmetic and copies ran while one was open for 0% -> 0% of each run, Pallas kernels for 7% -> 7%
where the time goes in v5:
time: 41.7 us; the launch traced here: 41.5 us
  blocking collectives  26.6 us (64%)
  Pallas kernels  7.94 us (19%)
  starting transfers between devices  3.33 us (8%)
  waiting for transfers between devices  2.87 us (7%)
  between operations  0.7 us (2%)
    all_to_all x1, blocking collectives, on_device(): parts = lax.all_to_all(packed, axes, 0, 0, tiled=True)  14.8 us
    all_to_all x1, blocking collectives, on_device(): total = lax.all_to_all(mine, axes, 0, 0, tiled=True)  9.91 us
    pallas_call x9, Pallas kernels, call(): pl.pallas_call(kernel, out_shape=out, in_specs=specs or [VMEM] * len(inpu...  7.94 us
    ppermute x1, starting transfers between devices, on_device(): lax.ppermute(send[0], 'space', pairs_of((size, GY), grid_z, 0))  3.06 us
    ppermute x1, waiting for transfers between devices, on_device(): lax.ppermute(send[0], 'space', pairs_of((size, GY), grid_z, 0))  2.34 us
    all_gather x1, blocking collectives, on_device(): lax.all_gather(send[1], 'space', axis_index_groups=inner + ends, tiled=True)  1.93 us
  transfers between devices with their start and end apart: 3, of which 2 were waited for; matrix products, arithmetic and copies ran while one was open for 0% of the time, Pallas kernels for 7%

profile of v5, /device:TPU:0, one launch (start us, length us, event | category | flops | bytes accessed | tf_op | source)
XLA Modules:
  0.0 41.5 jit_solution(6905306174691824753)
XLA Ops:
  0.6 1.2 %fetch.1 = (bf16[4,8,8,256]{3,2,1,0:T(8,128)(2,1)S(1)}, bf16[32,4,4,128]{3,2,1,0:T(4,128)(2,1)S(1)}, bf16[64,2,2,64]{3,2,1,0:T(2,128)(2,1)S(1)}, bf16[27,4,32]{2...) custom-call(bf16[1,2,4,8,8,256]{5,4,3,2,1,0:T(8,128)(2,1)} %refs_0_.1, ...), custom_call_target="tpu_custom_call" | custom-call | tf_op jit(solution)/shard_map/fetch/pallas_call | solution.py:370
  1.9 0.1 y_pack.1
  2.0 3.1 %collective-permute-start = (bf16[384,128]{1,0:T(8,128)(2,1)S(1)}, bf16[384,128]{1,0:T(8,128)(2,1)S(1)}, u32[]{:S(2)}, u32[]{:S(2)}) collective-permute-start(bf16[384,128]{1,0:T(8,128)(2,1)S(1)} %get-tuple-element.37), channel_id=1, source_target_pairs={{0,2},{1,3},{2,0},{3,1},{4,6},{5,7},{6,4},{7,5},{8,10},{9,11},{10,... | collective-permute-start | bytes 294920 | tf_op jit(solution)/shard_map/ppermute | solution.py:418
  5.1 1.9 %all_gather.3.rb_ref = bf16[768,128]{1,0:T(8,128)(2,1)S(1)} all-gather(bf16[384,128]{1,0:T(8,128)(2,1)S(1)} %get-tuple-element.38), channel_id=1, replica_groups={{2,4},{3,5},{6,8},{7,9},{10,12},{11,13},{0,1},{14,15},{18,20},{19,21},{..., dimensions={0}, use_global_device_ids=true | all-gather | bytes 294912 | tf_op jit(solution)/shard_map/all_gather | solution.py:419
  7.0 2.3 %collective-permute-done.ra_ref = bf16[384,128]{1,0:T(8,128)(2,1)S(1)} collective-permute-done((bf16[384,128]{1,0:T(8,128)(2,1)S(1)}, bf16[384,128]{1,0:T(8,128)(2,1)S(1)}, u32[]{:S(2)}, u32[]{:S(2)}) %collective-permute-start) | collective-permute-done | bytes 98336 | tf_op jit(solution)/shard_map/ppermute | solution.py:418
  9.3 0.2 z_pack.1
  9.5 0.1 collective-permute-start.1
  9.6 1.0 %prep.1 = (bf16[768,1024]{1,0:T(8,128)(2,1)S(1)}, bf16[432,2048]{1,0:T(8,128)(2,1)S(1)}, bf16[3,192,480]{2,1,0:T(8,128)(2,1)S(1)}, bf16[3,128,1152]{2,1,0:T(8,12...) custom-call(bf16[4,4,32,128]{3,2,1,0:T(8,128)(2,1)S(1)} %bitcast.24, ...), custom_call_target="tpu_custom_call" | custom-call | tf_op jit(solution)/shard_map/prep/pallas_call | solution.py:370
  10.6 0.5 %collective-permute-done.1.refs_4_.refs_5_ = bf16[960,128]{1,0:T(8,128)(2,1)S(1)} collective-permute-done((bf16[960,128]{1,0:T(8,128)(2,1)S(1)}, bf16[960,128]{1,0:T(8,128)(2,1)S(1)}, u32[]{:S(2)}, u32[]{:S(2)}) %collective-permute-start.1) | collective-permute-done | bytes 245792 | tf_op jit(solution)/shard_map/ppermute | solution.py:430
  11.1 2.3 %second_grads.1 = (bf16[768,1024]{1,0:T(8,128)(2,1)S(1)}, bf16[1152,768]{1,0:T(8,128)(2,1)S(1)}, f32[216,128]{1,0:T(8,128)S(1)}, f32[216,128]{1,0:T(8,128)S(1)}, f32[8,64]{1,0:T(8,128)S(1)}) custom-call(bf16[768,1024]{1,0:T(8,128)(2,1)S(1)} %get-tuple-element.45.refs_0_, ...), custom_call_target="tpu_custom_call", output_to_operand_aliasing={{0}: (0, {})} | custom-call | tf_op jit(solution)/shard_map/second_grads/pallas_call | solution.py:370
  13.4 0.2 collective-permute-start.2
  13.6 2.0 %first_grads.1 = (bf16[432,2048]{1,0:T(8,128)(2,1)S(1)}, f32[40,128]{1,0:T(8,128)S(1)}, f32[8,32]{1,0:T(8,128)S(1)}) custom-call(bf16[432,2048]{1,0:T(8,128)(2,1)S(1)} %get-tuple-element.53.refs_0_, bf16[1152,768]{1,0:T(8,128)(2,1)S(1)} %get-tuple-element.54.refs_1_, ...), custom_call_target="tpu_custom_call", output_to_operand_aliasing={{0}: (0, {})} | custom-call | tf_op jit(solution)/shard_map/first_grads/pallas_call | solution.py:370
  15.6 0.0 collective-permute-done.2.got_ref
  15.6 0.1 pack_grads.1
  15.7 14.8 %all_to_all.10.parts_ref = f32[32,8,128]{2,1,0:T(8,128)S(1)} all-to-all(f32[32,8,128]{2,1,0:T(8,128)S(1)} %pack_grads.1), channel_id=1, replica_groups=mesh['section'=2,'space'=16] {'section','space'}, dimensions={0} | all-to-all | bytes 262144 | tf_op jit(solution)/shard_map/all_to_all | solution.py:483
  30.6 9.9 %all_to_all.11.sum_ref = bf16[32,2,8,128]{3,2,1,0:T(8,128)(2,1)S(1)} all-to-all(bf16[32,2,8,128]{3,2,1,0:T(8,128)(2,1)S(1)} %sum_parts.1), channel_id=1, replica_groups=mesh['section'=2,'space'=16] {'section','space'}, dimensions={0} | all-to-all | bytes 262144 | tf_op jit(solution)/shard_map/all_to_all | solution.py:490
  40.5 1.0 %unpack.1 = (f32[27,4,32]{2,1,0:T(4,128)}, f32[1,32]{1,0:T(1,128)}, f32[864,64]{1,0:T(8,128)}, f32[1,64]{1,0:T(1,128)}) custom-call(bf16[32,2,8,128]{3,2,1,0:T(8,128)(2,1)S(1)} %all_to_all.11.sum_ref), custom_call_target="tpu_custom_call" | custom-call | tf_op jit(solution)/shard_map/unpack/pallas_call | solution.py:370
  (3 shorter events, 0.1 us)
Async XLA Ops:
  2.0 7.3 %collective-permute-start = (bf16[384,128]{1,0:T(8,128)(2,1)S(1)}, bf16[384,128]{1,0:T(8,128)(2,1)S(1)}, u32[]{:S(2)}, u32[]{:S(2)}) collective-permute-start(bf16[384,128]{1,0:T(8,128)(2,1)S(1)} %get-tuple-element.37), channel_id=1, source_target_pairs={{0,2},{1,3},{2,0},{3,1},{4,6},{5,7},{6,4},{7,5},{8,10},{9,11},{10,... | collective-permute-start | bytes 294920 | tf_op jit(solution)/shard_map/ppermute | solution.py:418
  9.5 1.6 %collective-permute-start.1 = (bf16[960,128]{1,0:T(8,128)(2,1)S(1)}, bf16[960,128]{1,0:T(8,128)(2,1)S(1)}, u32[]{:S(2)}, u32[]{:S(2)}) collective-permute-start(bf16[960,128]{1,0:T(8,128)(2,1)S(1)} %get-tuple-element.49), channel_id=1, source_target_pairs={{0,1},{1,0},{2,3},{3,2},{4,5},{5,4},{6,7},{7,6},{8,9},{9,8},{10,11... | collective-permute-start | bytes 737288 | tf_op jit(solution)/shard_map/ppermute | solution.py:430
  13.4 2.2 %collective-permute-start.2 = (f32[216,128]{1,0:T(8,128)S(1)}, f32[216,128]{1,0:T(8,128)S(1)}, u32[]{:S(2)}, u32[]{:S(2)}) collective-permute-start(f32[216,128]{1,0:T(8,128)S(1)} %get-tuple-element.51), channel_id=1, source_target_pairs={{0,1},{1,0},{2,3},{3,2},{4,5},{5,4},{6,7},{7,6},{8,9},{9,8},{10,11... | collective-permute-start | bytes 331784 | tf_op jit(solution)/shard_map/ppermute | solution.py:462

commit v6 on v5

--- a/solution.py
+++ b/solution.py
@@ -12,7 +12,7 @@
 BF = jnp.bfloat16
 F32 = jnp.float32
 LOW = np.float32(0.3) * np.float32(0.125)
-SPAN = 48
+PATCH = 432
 VMEM = pl.BlockSpec(memory_space=pltpu.VMEM)
 
 
@@ -28,11 +28,15 @@
 
 
 def place_of(flat):
-    block = lax.shift_right_logical(flat * 1366, 16)
-    r = flat - block * SPAN
-    chan = jnp.where(r < 32, lax.shift_right_logical(r, 3), r & 3)
-    plane = jnp.where(r < 32, (r & 7) + 1, jnp.where(r < 36, 0, jnp.where(r < 40, 9, -100)))
-    return block, chan, plane
+    own = flat < 288
+    block = jnp.where(
+        own, lax.shift_right_logical(flat, 5), lax.shift_right_logical(flat - 288, 4)
+    )
+    r = flat & 31
+    h = flat & 15
+    chan = jnp.where(own, lax.shift_right_logical(r, 3), h & 3)
+    rim = jnp.where(h < 4, 0, jnp.where(h < 8, 9, -100))
+    return block, chan, jnp.where(own, (r & 7) + 1, rim)
 
 
 def shifts(block):
@@ -143,29 +147,30 @@
         xs[row : row + 32, y * 128 : y * 128 + 128] = value
 
 
-def put_first(x0s, y, start, block):
+def put_first(x0s, y, rim, block):
+    size = block.shape[0]
     for c, value in enumerate(shifts(block)):
         for a in range(3):
             if 0 <= y - a < 8:
-                row = (a * 3 + c) * SPAN + start
-                x0s[row : row + block.shape[0], (y - a) * 256 : (y - a + 1) * 256] = value
+                row = (288 if rim else 0) + (a * 3 + c) * size
+                x0s[row : row + size, (y - a) * 256 : (y - a + 1) * 256] = value
 
 
 def prep(
     x1_ref, x0_ref, x1r_ref, x0r_ref, w1_ref, b1_ref, w2_ref, b2_ref,
-    xs, x0s, wb2, wd, wb0, b1_out, b2_out, w1f,
+    xs, x0s, wb2, wd, wrim, pre_out, b2_out, wb0, w1f,
 ):
     for y in range(4):
         for z in range(4):
             put_second(xs, y + 2, z + 2, x1_ref[y, z])
     for y in range(8):
         block = jnp.concatenate([x0_ref[i, y] for i in range(4)], axis=0)
-        put_first(x0s, y + 1, 0, block)
+        put_first(x0s, y + 1, False, block)
     for k, y in enumerate((0, 1, 6, 7)):
         for z in range(4):
             put_second(xs, y, z + 2, x1r_ref[k, z])
     for k, y in enumerate((0, 9)):
-        put_first(x0s, y, 0, x0r_ref[k])
+        put_first(x0s, y, False, x0r_ref[k])
     wb2[...] = jnp.zeros_like(wb2)
     wd[...] = jnp.zeros_like(wd)
     for a in range(3):
@@ -180,22 +185,28 @@
                     at = (z + b) * 192 + c * 64
                     wd[a, z * 32 : z * 32 + 32, at : at + 64] = value
     b2_out[...] = jnp.transpose(jnp.broadcast_to(b2_ref[...], (128, 64)))
-    b1_out[...] = jnp.transpose(jnp.broadcast_to(b1_ref[...], (128, 32)))
+    b1c = jnp.transpose(jnp.broadcast_to(b1_ref[...], (128, 32)))
     w1f[108:112, :] = jnp.zeros((4, 32), F32)
     for k in range(27):
         w1f[k * 4 : k * 4 + 4, :] = w1_ref[k].astype(F32)
     w1t = jnp.transpose(w1f[...]).astype(BF)
-    block, chan, plane = place_of(lax.broadcasted_iota(jnp.int32, (112, 9 * SPAN), 1))
-    row = lax.broadcasted_iota(jnp.int32, (112, 9 * SPAN), 0)
+    block, chan, plane = place_of(lax.broadcasted_iota(jnp.int32, (112, PATCH), 1))
+    row = lax.broadcasted_iota(jnp.int32, (112, PATCH), 0)
     third = lax.shift_right_logical(block * 11, 5)
     home = jnp.where(plane >= 0, third * 24 + block * 4 + chan, -100)
     spread = [dot(w1t, jnp.where(row == home + b * 12, 1.0, 0.0).astype(BF)) for b in range(3)]
-    zrow = place_of(lax.broadcasted_iota(jnp.int32, (32, 9 * SPAN), 1))[2]
+    zrow = place_of(lax.broadcasted_iota(jnp.int32, (32, PATCH), 1))[2]
     for z in range(8):
-        value = jnp.zeros((32, 9 * SPAN), F32)
+        value = jnp.zeros((32, PATCH), F32)
         for b in range(3):
             value = jnp.where(zrow == z + b, spread[b], value)
-        wb0[z * 32 : z * 32 + 32, :] = value.astype(BF)
+        wb0[z * 32 : z * 32 + 32, :] = value[:, :288].astype(BF)
+        if z in (0, 7):
+            wrim[z // 7 * 32 : z // 7 * 32 + 32, :] = value[:, 288:].astype(BF)
+    b1w = jnp.concatenate([jnp.concatenate([b1c, b1c], axis=1)] * 8, axis=0)
+    for y in range(8):
+        lanes = slice(y * 256, y * 256 + 256)
+        pre_out[:, lanes] = dot(wb0[...], x0s[:288, lanes]) + b1w
 
 
 def rims_of(grid_z, got):
@@ -210,9 +221,9 @@
 
 
 def second_grads(grid_z, kinds, *refs):
-    xs_in, wb2, b2_ref, g2y_ref = refs[:4]
-    rims = rims_of(grid_z, refs[4 : 4 + kinds])
-    xs, ds, keep_ref, send_ref, bias_ref, dz1 = refs[4 + kinds :]
+    xs_in, wb2, wd, b2_ref, g2y_ref = refs[:5]
+    rims = rims_of(grid_z, refs[5 : 5 + kinds])
+    xs, up, keep_ref, send_ref, bias_ref, dz1, ds = refs[5 + kinds :]
 
     for y in range(8):
         for p in range(2):
@@ -254,23 +265,23 @@
     line = dot_nt(jnp.ones((8, 512), BF), own)
     bias_ref[...] = sum(line[:, z * 64 : z * 64 + 64] for z in range(4))
     parts = []
+    first = lax.broadcasted_iota(jnp.int32, (288, 128), 1) < 64
     for a in range(3):
         lanes = slice((a + 1) * 128, (a + 5) * 128)
         full = dot_nt(xs[96:480, lanes], own[:128])
         full += dot_nt(xs[288:672, lanes], own[128:])
-        parts.append(full[:288, :64] + full[96:, 64:])
+        flip = pltpu.roll(full, 64, 1)
+        parts.append(jnp.where(first, full[:288] + flip[96:], flip[:288] + full[96:]))
     even = z_parity(grid_z) == 0
-    low = (parts[0][:216], jnp.concatenate([parts[0][216:], parts[1][:144]], axis=0))
-    high = (jnp.concatenate([parts[1][144:], parts[2][:72]], axis=0), parts[2][72:])
-    for k in range(2):
-        keep_ref[:216, k * 64 : k * 64 + 64] = jnp.where(even, low[k], high[k])
-        send_ref[:, k * 64 : k * 64 + 64] = jnp.where(even, high[k], low[k])
-
-
-def first_grads(grid_z, kinds, *refs):
-    x0s_in, ds, wd, wb0, b1_ref = refs[:5]
-    rims = rims_of(grid_z, refs[5 : 5 + kinds])
-    x0s, out_ref, line_ref, dz0, up = refs[5 + kinds :]
+    first = first[:216]
+    low = jnp.where(
+        first, parts[0][:216], jnp.concatenate([parts[0][216:], parts[1][:144]], axis=0)
+    )
+    high = jnp.where(
+        first, jnp.concatenate([parts[1][144:], parts[2][:72]], axis=0), parts[2][72:]
+    )
+    keep_ref[...] = jnp.where(even, low, high)
+    send_ref[...] = jnp.where(even, high, low)
 
     back = dot(wd[0], ds[:, :512])
     back += dot(wd[1], ds[:, 128:640])
@@ -279,20 +290,27 @@
     stack = [back[:, y * 128 : y * 128 + 128] for y in range(4)]
     up[...] = dot(jnp.concatenate(stack, axis=0), doubler(128))
 
+
+def first_grads(grid_z, kinds, *refs):
+    x0s_in, up, wrim, pre_ref = refs[:4]
+    rims = rims_of(grid_z, refs[4 : 4 + kinds])
+    x0s, out_ref, line_ref, dz0 = refs[4 + kinds :]
+
     ones = jnp.where(lax.broadcasted_iota(jnp.int32, (8, 256), 0) == 0, 1.0, 0.0)
     for y in range(10):
         halves = [rims(640 + y * 32 + h * 16, 16) for h in range(2)]
         low, high = (jnp.concatenate([h[k] for h in halves], axis=1) for k in range(2))
         pair = jnp.concatenate([low[:4].astype(F32), high[:4].astype(F32)], axis=0)
-        put_first(x0s, y, 32, jnp.concatenate([pair, ones], axis=0).astype(BF))
-
-    b1w = jnp.concatenate([b1_ref[...], b1_ref[...]], axis=1)
+        put_first(x0s, y, True, jnp.concatenate([pair, ones], axis=0).astype(BF))
+
     for y in range(8):
         lanes = slice(y * 256, y * 256 + 256)
-        pre = dot(wb0[...], x0s[:, lanes])
+        more = dot(wrim[...], x0s[288:, lanes])
         for z in range(8):
             at = (y // 2) * 128 + (z // 2) * 32
-            here = pre[z * 32 : z * 32 + 32] + b1w
+            here = pre_ref[z * 32 : z * 32 + 32, lanes]
+            if z in (0, 7):
+                here += more[z // 7 * 32 : z // 7 * 32 + 32]
             delta = up[at : at + 32, :] * jnp.where(here > 0, 0.125, LOW)
             dz0[z * 32 : z * 32 + 32, lanes] = delta.astype(BF)
 
@@ -305,17 +323,17 @@
     upper = (row[:, :128] & 2) == 2
     out_ref[36:, :] = jnp.zeros((4, 128), F32)
     for block in range(9):
-        edge = jnp.where(ends, full[block * SPAN + 32 : block * SPAN + 40], 0.0)
+        edge = jnp.where(ends, full[288 + block * 16 : 296 + block * 16], 0.0)
         edge = edge[:, :128] + edge[:, 128:]
         edge = pltpu.roll(edge[:4], 32, 1) + edge[4:]
         for i in range(4):
-            part = jnp.where(band, full[block * SPAN + i * 8 : block * SPAN + i * 8 + 8], 0.0)
+            part = jnp.where(band, full[block * 32 + i * 8 : block * 32 + i * 8 + 8], 0.0)
             part = part[:, :128] + part[:, 128:]
             part = jnp.where(odd, pltpu.roll(part, 96, 1), part)
             part = jnp.where(upper, pltpu.roll(part, 64, 1), part)
             part = jnp.sum(part, axis=0, keepdims=True) + edge[i : i + 1]
             out_ref[block * 4 + i : block * 4 + i + 1, :] = part
-    line = full[4 * SPAN + 40 : 4 * SPAN + 48]
+    line = full[360:368]
     line_ref[...] = sum(line[:, z * 32 : z * 32 + 32] for z in range(8))
 
 
@@ -344,12 +362,8 @@
         out_ref[k, 1] = sums[1].astype(BF)
 
 
-def unpack(count, deep, sum_ref, g1_ref, b1_ref, g2_ref, b2_ref, flat):
-    for half in range(2):
-        for k in range(deep - 1):
-            flat[k * count : (k + 1) * count, :] = sum_ref[:, half, k, :].astype(F32)
-        g2_ref[half * 432 : half * 432 + 216, :] = flat[:216, :64]
-        g2_ref[half * 432 + 216 : half * 432 + 432, :] = flat[:216, 64:]
+def unpack(count, deep, sum_ref, *refs):
+    outs, (g1_ref, b1_ref, g2_ref, b2_ref, flat, sems) = refs[:4], refs[4:]
     flat[:count, :] = sum_ref[:, 0, deep - 1, :].astype(F32)
     for a in range(3):
         for b in range(3):
@@ -364,14 +378,33 @@
                     g1_ref[a * 9 + b * 3 + c, i : i + 1] = value
     b2_ref[...] = flat[27:28, :64]
     b1_ref[...] = flat[27:28, 64:96]
-
-
-def call(kernel, out, inputs, scratch=(), name=None, room=8, specs=None, alias=None):
+    copies = [
+        pltpu.make_async_copy(g1_ref, outs[0], sems.at[0]),
+        pltpu.make_async_copy(b1_ref, outs[1], sems.at[1]),
+        pltpu.make_async_copy(b2_ref, outs[3], sems.at[2]),
+    ]
+    for copy in copies:
+        copy.start()
+    for half in range(2):
+        for k in range(deep - 1):
+            at = (half * deep + k) * count
+            flat[at : at + count, :] = sum_ref[:, half, k, :].astype(F32)
+        at = half * deep * count
+        g2_ref[half * 432 : half * 432 + 216, :] = flat[at : at + 216, :64]
+        g2_ref[half * 432 + 216 : half * 432 + 432, :] = flat[at : at + 216, 64:]
+        rows = slice(half * 432, half * 432 + 432)
+        copies.append(pltpu.make_async_copy(g2_ref.at[rows], outs[2].at[rows], sems.at[3 + half]))
+        copies[-1].start()
+    for copy in copies:
+        copy.wait()
+
+
+def call(kernel, out, inputs, scratch=(), name=None, room=8, specs=None, outs=None, alias=None):
     return pl.pallas_call(
         kernel,
         out_shape=out,
         in_specs=specs or [VMEM] * len(inputs),
-        out_specs=jax.tree.map(lambda _: VMEM, out),
+        out_specs=outs or jax.tree.map(lambda _: VMEM, out),
         scratch_shapes=list(scratch),
         input_output_aliases=alias or {},
         name=name,
@@ -430,41 +463,41 @@
         lax.ppermute(v, "space", pairs_of((size, grid_z), 1, k))
         for k, v in enumerate(wide[3:])
     ]
-    xs, x0s, wb2, wd, wb0, b1, b2 = call(
+    xs, x0s, wb2, wd, wrim, pre, b2 = call(
         prep,
         (
             shaped(768, 1024),
-            shaped(9 * SPAN, 2048),
+            shaped(PATCH, 2048),
             shaped(3, 192, 480),
             shaped(3, 128, 1152),
-            shaped(256, 9 * SPAN),
-            shaped(32, 128, dtype=F32),
+            shaped(64, 144),
+            shaped(256, 2048, dtype=F32),
             shaped(64, 128, dtype=F32),
         ),
         (x1, x0, wide[0], wide[2], w1, b1, w2, b2),
-        scratch=(pltpu.VMEM((112, 32), F32),),
+        scratch=(pltpu.VMEM((256, 288), BF), pltpu.VMEM((112, 32), F32)),
         name="prep",
     )
-    xs, ds, keep, swap, line_two = call(
+    xs, up, keep, swap, line_two = call(
         functools.partial(second_grads, grid_z, kinds),
         (
             shaped(768, 1024),
-            shaped(1152, 768),
+            shaped(512, 256, dtype=F32),
             shaped(216, 128, dtype=F32),
             shaped(216, 128, dtype=F32),
             shaped(8, 64, dtype=F32),
         ),
-        (xs, wb2, b2, wide[1], *rims),
-        scratch=(pltpu.VMEM((384, 768), BF),),
+        (xs, wb2, wd, b2, wide[1], *rims),
+        scratch=(pltpu.VMEM((384, 768), BF), pltpu.VMEM((1152, 768), BF)),
         alias={0: 0},
         name="second_grads",
     )
     swap = lax.ppermute(swap, "space", [(k, k ^ 1) for k in range(size)])
     x0s, part_one, line_one = call(
         functools.partial(first_grads, grid_z, kinds),
-        (shaped(9 * SPAN, 2048), shaped(40, 128, dtype=F32), shaped(8, 32, dtype=F32)),
-        (x0s, ds, wd, wb0, b1, *rims),
-        scratch=(pltpu.VMEM((256, 2048), BF), pltpu.VMEM((512, 256), F32)),
+        (shaped(PATCH, 2048), shaped(40, 128, dtype=F32), shaped(8, 32, dtype=F32)),
+        (x0s, up, wrim, pre, *rims),
+        scratch=(pltpu.VMEM((256, 2048), BF),),
         alias={0: 0},
         name="first_grads",
     )
@@ -497,7 +530,15 @@
             shaped(1, 64, dtype=F32),
         ),
         (total,),
-        scratch=lines,
+        scratch=(
+            pltpu.VMEM((27, 4, 32), F32),
+            pltpu.VMEM((1, 32), F32),
+            pltpu.VMEM((864, 64), F32),
+            pltpu.VMEM((1, 64), F32),
+            pltpu.VMEM((2 * deep * count, 128), F32),
+            pltpu.SemaphoreType.DMA((5,)),
+        ),
+        outs=(pl.BlockSpec(memory_space=pltpu.HBM),) * 4,
         name="unpack",
     )
     g1 = jnp.transpose(g1.reshape(3, 3, 3, 4, 32), (4, 3, 0, 1, 2))

time: 41.7 us -> 41.6 us (level)
  transfers between devices with their start and end apart: 3 -> 3, of which waited for: 2 -> 2; matrix products, arithmetic and copies ran while one was open for 0% -> 0% of each run, Pallas kernels for 7% -> 6%
where the time goes in v6:
time: 41.6 us; the launch traced here: 41.4 us
  blocking collectives  26.6 us (64%)
  Pallas kernels  7.93 us (19%)
  starting transfers between devices  3.58 us (9%)
  waiting for transfers between devices  2.46 us (6%)
  between operations  0.7 us (2%)
    all_to_all x1, blocking collectives, on_device(): parts = lax.all_to_all(packed, axes, 0, 0, tiled=True)  14.8 us
    all_to_all x1, blocking collectives, on_device(): total = lax.all_to_all(mine, axes, 0, 0, tiled=True)  9.91 us
    pallas_call x9, Pallas kernels, call(): pl.pallas_call(kernel, out_shape=out, in_specs=specs or [VMEM] * len(inpu...  7.93 us
    ppermute x1, starting transfers between devices, on_device(): lax.ppermute(send[0], 'space', pairs_of((size, GY), grid_z, 0))  3.06 us
    ppermute x1, waiting for transfers between devices, on_device(): lax.ppermute(send[0], 'space', pairs_of((size, GY), grid_z, 0))  2.34 us
    all_gather x1, blocking collectives, on_device(): lax.all_gather(send[1], 'space', axis_index_groups=inner + ends, tiled=True)  1.93 us
  transfers between devices with their start and end apart: 3, of which 2 were waited for; matrix products, arithmetic and copies ran while one was open for 0% of the time, Pallas kernels for 6%

profile of v6, /device:TPU:0, one launch (start us, length us, event | category | flops | bytes accessed | tf_op | source)
XLA Modules:
  0.0 41.4 jit_solution(14478532117401347599)
XLA Ops:
  0.6 1.2 %fetch.1 = (bf16[4,8,8,256]{3,2,1,0:T(8,128)(2,1)S(1)}, bf16[32,4,4,128]{3,2,1,0:T(4,128)(2,1)S(1)}, bf16[64,2,2,64]{3,2,1,0:T(2,128)(2,1)S(1)}, bf16[27,4,32]{2...) custom-call(bf16[1,2,4,8,8,256]{5,4,3,2,1,0:T(8,128)(2,1)} %refs_0_.1, ...), custom_call_target="tpu_custom_call" | custom-call | tf_op jit(solution)/shard_map/fetch/pallas_call | solution.py:403
  1.9 0.1 y_pack.1
  2.0 3.1 %collective-permute-start = (bf16[384,128]{1,0:T(8,128)(2,1)S(1)}, bf16[384,128]{1,0:T(8,128)(2,1)S(1)}, u32[]{:S(2)}, u32[]{:S(2)}) collective-permute-start(bf16[384,128]{1,0:T(8,128)(2,1)S(1)} %get-tuple-element.37), channel_id=1, source_target_pairs={{0,2},{1,3},{2,0},{3,1},{4,6},{5,7},{6,4},{7,5},{8,10},{9,11},{10,... | collective-permute-start | bytes 294920 | tf_op jit(solution)/shard_map/ppermute | solution.py:451
  5.1 1.9 %all_gather.3.rb_ref = bf16[768,128]{1,0:T(8,128)(2,1)S(1)} all-gather(bf16[384,128]{1,0:T(8,128)(2,1)S(1)} %get-tuple-element.38), channel_id=1, replica_groups={{2,4},{3,5},{6,8},{7,9},{10,12},{11,13},{0,1},{14,15},{18,20},{19,21},{..., dimensions={0}, use_global_device_ids=true | all-gather | bytes 294912 | tf_op jit(solution)/shard_map/all_gather | solution.py:452
  7.0 2.3 %collective-permute-done.ra_ref = bf16[384,128]{1,0:T(8,128)(2,1)S(1)} collective-permute-done((bf16[384,128]{1,0:T(8,128)(2,1)S(1)}, bf16[384,128]{1,0:T(8,128)(2,1)S(1)}, u32[]{:S(2)}, u32[]{:S(2)}) %collective-permute-start) | collective-permute-done | bytes 98336 | tf_op jit(solution)/shard_map/ppermute | solution.py:451
  9.3 0.2 z_pack.1
  9.5 0.1 collective-permute-start.1
  9.6 1.4 %prep.1 = (bf16[768,1024]{1,0:T(8,128)(2,1)S(1)}, bf16[432,2048]{1,0:T(8,128)(2,1)S(1)}, bf16[3,192,480]{2,1,0:T(8,128)(2,1)S(1)}, bf16[3,128,1152]{2,1,0:T(8,12...) custom-call(bf16[4,4,32,128]{3,2,1,0:T(8,128)(2,1)S(1)} %bitcast.24, ...), custom_call_target="tpu_custom_call" | custom-call | tf_op jit(solution)/shard_map/prep/pallas_call | solution.py:403
  11.0 0.1 collective-permute-done.1.refs_5_.refs_4_
  11.1 2.8 %second_grads.1 = (bf16[768,1024]{1,0:T(8,128)(2,1)S(1)}, f32[512,256]{1,0:T(8,128)S(1)}, f32[216,128]{1,0:T(8,128)S(1)}, f32[216,128]{1,0:T(8,128)S(1)}, f32[8,64]{1,0:T(8,128)S(1)}) custom-call(bf16[768,1024]{1,0:T(8,128)(2,1)S(1)} %get-tuple-element.45.refs_0_, ...), custom_call_target="tpu_custom_call", output_to_operand_aliasing={{0}: (0, {})} | custom-call | tf_op jit(solution)/shard_map/second_grads/pallas_call | solution.py:403
  14.0 0.5 %collective-permute-start.2 = (f32[216,128]{1,0:T(8,128)S(1)}, f32[216,128]{1,0:T(8,128)S(1)}, u32[]{:S(2)}, u32[]{:S(2)}) collective-permute-start(f32[216,128]{1,0:T(8,128)S(1)} %get-tuple-element.52), channel_id=1, source_target_pairs={{0,1},{1,0},{2,3},{3,2},{4,5},{5,4},{6,7},{7,6},{8,9},{9,8},{10,11... | collective-permute-start | bytes 331784 | tf_op jit(solution)/shard_map/ppermute | solution.py:495
  14.4 1.1 %first_grads.1 = (bf16[432,2048]{1,0:T(8,128)(2,1)S(1)}, f32[40,128]{1,0:T(8,128)S(1)}, f32[8,32]{1,0:T(8,128)S(1)}) custom-call(bf16[432,2048]{1,0:T(8,128)(2,1)S(1)} %get-tuple-element.54.refs_0_, f32[512,256]{1,0:T(8,128)S(1)} %get-tuple-element.55.refs_1_, bf16[64,144]{1,0:T(8,128)(2,1)S(1)} %get-tuple-element.56.refs_2_, ...), custom_call_target="tpu_custom_call", output_to_operand_aliasing={{0}: (0, {})} | custom-call | tf_op jit(solution)/shard_map/first_grads/pallas_call | solution.py:403
  15.5 0.0 collective-permute-done.2.got_ref
  15.5 0.1 pack_grads.1
  15.6 14.8 %all_to_all.10.parts_ref = f32[32,8,128]{2,1,0:T(8,128)S(1)} all-to-all(f32[32,8,128]{2,1,0:T(8,128)S(1)} %pack_grads.1), channel_id=1, replica_groups=mesh['section'=2,'space'=16] {'section','space'}, dimensions={0} | all-to-all | bytes 262144 | tf_op jit(solution)/shard_map/all_to_all | solution.py:516
  30.4 9.9 %all_to_all.11.sum_ref = bf16[32,2,8,128]{3,2,1,0:T(8,128)(2,1)S(1)} all-to-all(bf16[32,2,8,128]{3,2,1,0:T(8,128)(2,1)S(1)} %sum_parts.1), channel_id=1, replica_groups=mesh['section'=2,'space'=16] {'section','space'}, dimensions={0} | all-to-all | bytes 262144 | tf_op jit(solution)/shard_map/all_to_all | solution.py:523
  40.4 1.0 %unpack.1 = (f32[27,4,32]{2,1,0:T(4,128)}, f32[1,32]{1,0:T(1,128)}, f32[864,64]{1,0:T(8,128)}, f32[1,64]{1,0:T(1,128)}) custom-call(bf16[32,2,8,128]{3,2,1,0:T(8,128)(2,1)S(1)} %all_to_all.11.sum_ref), custom_call_target="tpu_custom_call" | custom-call | tf_op jit(solution)/shard_map/unpack/pallas_call | solution.py:403
  (3 shorter events, 0.1 us)
Async XLA Ops:
  2.0 7.3 %collective-permute-start = (bf16[384,128]{1,0:T(8,128)(2,1)S(1)}, bf16[384,128]{1,0:T(8,128)(2,1)S(1)}, u32[]{:S(2)}, u32[]{:S(2)}) collective-permute-start(bf16[384,128]{1,0:T(8,128)(2,1)S(1)} %get-tuple-element.37), channel_id=1, source_target_pairs={{0,2},{1,3},{2,0},{3,1},{4,6},{5,7},{6,4},{7,5},{8,10},{9,11},{10,... | collective-permute-start | bytes 294920 | tf_op jit(solution)/shard_map/ppermute | solution.py:451
  9.5 1.6 %collective-permute-start.1 = (bf16[960,128]{1,0:T(8,128)(2,1)S(1)}, bf16[960,128]{1,0:T(8,128)(2,1)S(1)}, u32[]{:S(2)}, u32[]{:S(2)}) collective-permute-start(bf16[960,128]{1,0:T(8,128)(2,1)S(1)} %get-tuple-element.50), channel_id=1, source_target_pairs={{0,1},{1,0},{2,3},{3,2},{4,5},{5,4},{6,7},{7,6},{8,9},{9,8},{10,11... | collective-permute-start | bytes 737288 | tf_op jit(solution)/shard_map/ppermute | solution.py:463
  14.0 1.5 %collective-permute-start.2 = (f32[216,128]{1,0:T(8,128)S(1)}, f32[216,128]{1,0:T(8,128)S(1)}, u32[]{:S(2)}, u32[]{:S(2)}) collective-permute-start(f32[216,128]{1,0:T(8,128)S(1)} %get-tuple-element.52), channel_id=1, source_target_pairs={{0,1},{1,0},{2,3},{3,2},{4,5},{5,4},{6,7},{7,6},{8,9},{9,8},{10,11... | collective-permute-start | bytes 331784 | tf_op jit(solution)/shard_map/ppermute | solution.py:495
